TPU v7x, 128 devices: a whole 4x4x4 slice. The times are simulated.
128 devices in a mesh: grp: 4 (over z), sub: 32 (over y, x, core).
Axes of the slice: x: 4, y: 4, z: 4, core: 2. Of those that a mesh axis runs over, the one named last changes fastest.
Arguments:
- points: bfloat16 [524288, 256], P(('grp', 'sub'))
- weights: bfloat16 [64, 524288], P(None, ('grp', 'sub')), may hold values from -6 to 6
- near: int32 [1024, 8], replicated, may hold values from 0 to 1023, as said below
- counts: int32 [1024], replicated, may hold values from 2 to 8, as said below
- skel_leaf: int32 [1024, 256], P(('grp', 'sub')), may hold values from 0 to 511, as said below
- skel_local: int32 [896, 256], P(('grp', 'sub')), may hold values from 0 to 511, as said below
- skel_upper: int32 [126, 256], replicated, may hold values from 0 to 511, as said below
Outputs:
- spread: float32 [64, 524288], P(None, ('grp', 'sub'))
Inputs may be any that keep to these rules, and one draw needn't show every extreme that they name: `near`: slot 0 of a leaf's row is the leaf itself; the other entries of a row are different leaves of other devices with the same index of grp. All slots of the rows of one device name at most one leaf of any other device. `counts`: the live slots over the leaves of one device number at most 48, and exactly 48 on one device. `skel_leaf`: the entries of a row are different. `skel_local`: the entries of a row are different. `skel_upper`: the entries of a row are different.
All inputs are finite; a program needn't handle non-finite values.
Results may differ from a plain program's by a relative error of at most 0.0023.
Values may be sent and summed in bfloat16 or wider, within the bound.
No kernel may reach another device: no remote copies, remote signals or barrier semaphores. Data moves between devices by JAX's collectives and lax.ppermute only.
A program may use at most 128 MiB of HBM per device.

v0:
```python
import functools
import math

import jax
import jax.numpy as jnp
import numpy as np
from jax import lax
from jax.experimental import pallas as pl
from jax.experimental.pallas import tpu as pltpu
from jax.sharding import PartitionSpec as P

F32 = jnp.float32
BF16 = jnp.bfloat16
LOG2E = 1.4426950408889634
NT = (((1,), (1,)), ((), ()))
LAST_ROWS = 256
GROUP = 1


def call(kernel, name, flops, exps, nbytes, vmem=12, **kw):
    return pl.pallas_call(
        kernel,
        name=name,
        cost_estimate=pl.CostEstimate(flops=flops, bytes_accessed=nbytes, transcendentals=exps),
        compiler_params=pltpu.CompilerParams(vmem_limit_bytes=vmem * 2**20),
        **kw,
    )


def in_hbm(array):
    return pltpu.with_memory_space_constraint(array, pltpu.HBM)


def dot(a, b):
    return jnp.dot(a, b, preferred_element_type=F32)


def dot_nt(a, b):
    return lax.dot_general(a, b, NT, preferred_element_type=F32)


def half_exponents(block):
    sharpness = math.sqrt(block.shape[-1] / 8.0)
    wide = block.astype(F32)
    norms = jnp.sum(wide * wide, axis=-1, keepdims=True)
    return LOG2E * (sharpness * (1.0 - norms) - 0.25)


def as_row(column):
    rows = column.shape[0]
    return jnp.transpose(jnp.broadcast_to(column, (rows, 128)))[0:1, :]


def kappa_of(inner, width, left_half, right_half_row):
    scale = LOG2E * 2.0 * math.sqrt(width / 8.0)
    return jnp.exp2(inner * scale + left_half + right_half_row)


def kappa(left, right, left_half, right_half_row):
    return kappa_of(dot_nt(left, right), left.shape[-1], left_half, right_half_row)


def one_hot(chosen_row, pool):
    rank = chosen_row.shape[1]
    spread = jnp.transpose(jnp.broadcast_to(chosen_row, (128, rank)).astype(F32)).astype(jnp.int32)
    lanes = lax.broadcasted_iota(jnp.int32, (rank, 128), 1)
    pieces = [
        jnp.where(spread == lanes + 128 * j, 1.0, 0.0).astype(BF16) for j in range(pool // 128)
    ]
    return jnp.concatenate(pieces, axis=1)


def score_pieces(rows, classes, width):
    pieces = []
    for column in range(0, rows, width):
        row = rows + column * classes // width
        if rows - column >= width:
            pieces.append((column, width, 0, classes, row, 0))
        else:
            half = classes // 2
            pieces.append((column, width // 2, 0, half, row, 0))
            pieces.append((column, width // 2, half, half, row, width // 2))
    return pieces


def pack_kernel(leaf_size, first, rows, chosen, points_ref, weights_ref, out_ref, sems):
    classes = weights_ref.shape[0]
    pieces = score_pieces(rows, classes, points_ref.shape[1])

    def copies(j):
        start = pl.multiple_of(chosen[j] * leaf_size + first, 128)
        made = [
            pltpu.make_async_copy(
                points_ref.at[pl.ds(start, rows), :],
                out_ref.at[j, pl.ds(0, rows), :],
                sems.at[j, 0],
            )
        ]
        for number, (column, columns, from_class, count, row, lane) in enumerate(pieces):
            made.append(
                pltpu.make_async_copy(
                    weights_ref.at[
                        pl.ds(from_class, count),
                        pl.ds(pl.multiple_of(start + column, 128), columns),
                    ],
                    out_ref.at[j, pl.ds(row, count), pl.ds(lane, columns)],
                    sems.at[j, 1 + number],
                )
            )
        return made

    def start(j, carry):
        @pl.when(chosen[j] >= 0)
        def _():
            for copy in copies(j):
                copy.start()

        return carry

    def finish(j, carry):
        @pl.when(chosen[j] >= 0)
        def _():
            for copy in copies(j):
                copy.wait()

        return carry

    lax.fori_loop(0, out_ref.shape[0], start, 0)
    lax.fori_loop(0, out_ref.shape[0], finish, 0)


def pack(chosen, points, weights, leaf_size, first, rows):
    classes, width = weights.shape[0], points.shape[1]
    shape = (chosen.shape[0], rows + rows * classes // width, width)
    return call(
        functools.partial(pack_kernel, leaf_size, first, rows),
        "pack",
        0,
        0,
        2 * math.prod(shape) * 2,
        out_shape=pltpu.HBM(shape, BF16),
        grid_spec=pltpu.PrefetchScalarGridSpec(
            num_scalar_prefetch=1,
            grid=(1,),
            in_specs=[
                pl.BlockSpec(points.shape, lambda i, c: (0, 0)),
                pl.BlockSpec(weights.shape, lambda i, c: (0, 0)),
            ],
            out_specs=pl.BlockSpec(memory_space=pltpu.HBM),
            scratch_shapes=[
                pltpu.SemaphoreType.DMA((shape[0], 1 + len(score_pieces(rows, classes, width))))
            ],
        ),
    )(chosen, in_hbm(points), in_hbm(weights))


def leaf_kernel(
    points_ref,
    weights_ref,
    chosen_ref,
    own_ref,
    skel_ref,
    up_ref,
    summary_ref,
    target_ref,
    half_ref,
):
    leaf = pl.program_id(0)
    block = points_ref[...]
    turned = jnp.transpose(block)
    target_ref[0] = turned
    leaf_size = block.shape[0]
    inverse_leaf = 1.0 / math.sqrt(leaf_size)
    half = half_exponents(block)
    half_row = as_row(half)
    half_ref[0] = half_row
    tile = kappa_of(dot(block, turned), block.shape[1], half, half_row)
    rows = lax.broadcasted_iota(jnp.int32, tile.shape, 0)
    columns = lax.broadcasted_iota(jnp.int32, tile.shape, 1)
    tile = jnp.where(rows == columns, 0.0, tile).astype(BF16)
    own = dot(weights_ref[...], tile) * inverse_leaf
    own_ref[...] = own
    chosen = chosen_ref[pl.ds(leaf, 1), :]
    rank = chosen.shape[1]
    skel_ref[0] = dot(one_hot(chosen, leaf_size), block).astype(BF16)
    places = lax.broadcasted_iota(jnp.int32, (leaf_size, rank), 0)
    columns_of = jnp.where(places == chosen, 1.0, 0.0).astype(BF16)
    up_ref[0] = dot(tile, columns_of).astype(BF16)
    summary_ref[0] = dot(own.astype(BF16), columns_of).astype(BF16)


def leaf_level(points, weights, skel_leaf):
    leaves, rank = skel_leaf.shape
    classes = weights.shape[0]
    width = points.shape[1]
    size = points.shape[0] // leaves
    return call(
        leaf_kernel,
        "leaf",
        leaves * 2 * size * (size * (width + classes + rank) + rank * width + classes * rank),
        leaves * size * size,
        8 * 2**20,
        out_shape=(
            pltpu.HBM(weights.shape, F32),
            jax.ShapeDtypeStruct((leaves, rank, width), BF16),
            pltpu.HBM((leaves, size, rank), BF16),
            jax.ShapeDtypeStruct((leaves, classes, rank), BF16),
            pltpu.HBM((leaves, width, size), BF16),
            pltpu.HBM((leaves, 1, size), F32),
        ),
        grid=(leaves,),
        in_specs=[
            pl.BlockSpec((size, width), lambda i: (i, 0)),
            pl.BlockSpec((classes, size), lambda i: (0, i)),
            pl.BlockSpec((leaves, rank), lambda i: (0, 0)),
        ],
        out_specs=(
            pl.BlockSpec((classes, size), lambda i: (0, i)),
            pl.BlockSpec((1, rank, width), lambda i: (i, 0, 0)),
            pl.BlockSpec((1, size, rank), lambda i: (i, 0, 0)),
            pl.BlockSpec((1, classes, rank), lambda i: (i, 0, 0)),
            pl.BlockSpec((1, width, size), lambda i: (i, 0, 0)),
            pl.BlockSpec((1, 1, size), lambda i: (i, 0, 0)),
        ),
    )(points, weights, skel_leaf)


def subtree_kernel(count, inner, states, rows, *refs):
    chosen_ref = refs[0]
    inputs = refs[1 : len(refs) - 5]
    lifted_ref, terms_ref, state_ref, nodes, sums = refs[len(refs) - 5 :]
    _, rank, width = nodes.shape
    classes = sums.shape[1]
    inverse_rank = 1.0 / rank
    inverse_pair = 1.0 / (math.sqrt(2.0) * rank)
    if states == 0:
        nodes[pl.ds(0, count)] = inputs[0][...]
        sums[pl.ds(0, count)] = inputs[1][...]
    else:
        for mask in range(count):
            place = lax.bitwise_xor(rows[inner], mask)
            nodes[place] = inputs[mask][pl.ds(0, rank), :]
            sums[place] = inputs[mask][pl.ds(rank, classes), :]

    def pair(i, even, odd, even_half, odd_half):
        tile = kappa(even, odd, even_half, as_row(odd_half)).astype(BF16)
        terms_ref[2 * i] = dot_nt(sums[2 * i + 1], tile) * inverse_rank
        terms_ref[2 * i + 1] = dot(sums[2 * i], tile) * inverse_rank

    def step(i, carry):
        even, odd = nodes[2 * i], nodes[2 * i + 1]
        child = jnp.concatenate([even, odd], axis=0)
        chosen = chosen_ref[pl.ds(rows[i], 1), :]
        half = half_exponents(child)
        parent = dot(one_hot(chosen, 2 * rank), child).astype(BF16)
        lifted = kappa(child, parent, half, as_row(half_exponents(parent)))
        same = lax.broadcasted_iota(jnp.int32, lifted.shape, 0) == chosen
        lifted = jnp.where(same, 0.0, lifted).astype(BF16)
        lifted_ref[i] = lifted
        summed = dot(sums[2 * i], lifted[:rank]) + dot(sums[2 * i + 1], lifted[rank:])
        nodes[count + i] = parent
        sums[count + i] = (summed * inverse_pair).astype(BF16)
        pair(i, even, odd, half[:rank], half[rank:])
        return carry

    lax.fori_loop(0, inner, step, 0)
    if inner == count - 1:
        state_ref[pl.ds(0, rank), :] = nodes[count + inner - 1]
        state_ref[pl.ds(rank, classes), :] = sums[count + inner - 1]
    else:
        even, odd = nodes[2 * inner], nodes[2 * inner + 1]
        pair(inner, even, odd, half_exponents(even), half_exponents(odd))
        state_ref[...] = jnp.zeros_like(state_ref)


def subtree(name, count, inner, states, rows, table, inputs, classes):
    rank = table.shape[1]
    width = inputs[0].shape[-1]

    def whole(array):
        zeros = (0,) * len(array.shape)
        return pl.BlockSpec(array.shape, lambda i, r: zeros)

    shapes = (
        pltpu.HBM((inner, 2 * rank, rank), BF16),
        pltpu.HBM((2 * count - 2, classes, rank), F32),
        jax.ShapeDtypeStruct((rank + classes, width), BF16),
    )
    return call(
        functools.partial(subtree_kernel, count, inner, states),
        name,
        inner * 2 * rank * rank * (5 * width + 4 * classes),
        inner * 3 * rank * rank,
        6 * 2**20,
        vmem=16,
        out_shape=shapes,
        grid_spec=pltpu.PrefetchScalarGridSpec(
            num_scalar_prefetch=1,
            grid=(1,),
            in_specs=[whole(table)] + [whole(array) for array in inputs],
            out_specs=tuple(whole(shape) for shape in shapes),
            scratch_shapes=[
                pltpu.VMEM((2 * count, rank, width), BF16),
                pltpu.VMEM((2 * count, classes, rank), BF16),
            ],
        ),
    )(in_hbm(rows), in_hbm(table), *inputs)


def path_of(place, count):
    numbers = [place]
    while 2 ** len(numbers) < count:
        numbers.append(count + (numbers[-1] >> 1))
    return numbers


def place_table(steps):
    devices = 1 << sum(steps)
    table = []
    for device in range(devices):
        parts, paths, height = [], [], 0
        for number, step in enumerate(steps):
            rows = []
            for u in range(height + 1, height + step + 1):
                under = 1 << (height + step - u)
                base = devices - (devices >> u - 1) + (device >> height + step) * under
                rows += [base + i for i in range(under)]
            if number + 1 == len(steps):
                rows = rows[:-1]
            place = device >> height & (1 << step) - 1
            parts.append(rows + [place])
            paths.insert(0, path_of(place, 1 << step)[::-1])
            height += step
        parts.append([node for path in paths for node in path])
        table.append([number for part in parts for number in part])
    starts = np.cumsum([0] + [len(part) for part in parts]).tolist()
    return np.array(table, np.int32), starts, tuple(len(path) for path in paths)


def down_kernel(path, stages, numbers, *refs):
    lifted_hbm, terms_hbm, up_hbm, own_hbm, out_ref = refs[2 * stages : 2 * stages + 5]
    lifted_ref, terms_ref, up_ref, path_lifted, path_terms, values = refs[2 * stages + 5 : -3]
    path_sems, up_sems, sems = refs[-3:]
    inner, _, rank = lifted_ref.shape
    leaves, size, _ = up_ref.shape
    inverse_rank = 1.0 / rank

    path_copies = []
    for stage, steps in enumerate(path):
        for _ in range(steps):
            at = len(path_copies)
            node = numbers[at]
            copies = [
                pltpu.make_async_copy(
                    refs[2 * stage + 1].at[node], path_terms.at[at], path_sems.at[at, 0]
                )
            ]
            if at > 0:
                half = pl.ds(pl.multiple_of((node & 1) * rank, rank), rank)
                copies.append(
                    pltpu.make_async_copy(
                        refs[2 * stage].at[node >> 1, half, :],
                        path_lifted.at[at],
                        path_sems.at[at, 1],
                    )
                )
            path_copies.append(copies)
    local_copies = [
        pltpu.make_async_copy(terms_hbm, terms_ref, sems.at[0]),
        pltpu.make_async_copy(lifted_hbm, lifted_ref, sems.at[1]),
    ]
    own_copy = pltpu.make_async_copy(own_hbm, out_ref, sems.at[2])
    up_copies = [
        pltpu.make_async_copy(up_hbm.at[leaf], up_ref.at[leaf], up_sems.at[leaf])
        for leaf in range(leaves)
    ]
    for copies in path_copies:
        for copy in copies:
            copy.start()
    for copy in local_copies + [own_copy] + up_copies:
        copy.start()

    value = None
    for at, copies in enumerate(path_copies):
        for copy in copies:
            copy.wait()
        term = path_terms[at]
        if at > 0:
            term = term + dot_nt(value, path_lifted[at]) * inverse_rank
        value = term.astype(BF16)
    values[2 * leaves - 2] = value
    for copy in local_copies:
        copy.wait()

    def lower(step, carry):
        i = inner - 1 - step
        down = dot_nt(values[leaves + i], lifted_ref[i]) * inverse_rank
        values[2 * i] = (terms_ref[2 * i] + down[:, :rank]).astype(BF16)
        values[2 * i + 1] = (terms_ref[2 * i + 1] + down[:, rank:]).astype(BF16)
        return carry

    lax.fori_loop(0, inner, lower, 0)
    own_copy.wait()
    for leaf in range(leaves):
        up_copies[leaf].wait()
        columns = pl.ds(leaf * size, size)
        out_ref[:, columns] += dot_nt(values[leaf], up_ref[leaf]) * inverse_rank


def down(numbers, path, stages, lifted, terms, up, own):
    leaves, size, rank = up.shape
    classes = own.shape[0]
    inputs = [array for stage in stages for array in stage] + [lifted, terms, up, own]
    hbm = pl.BlockSpec(memory_space=pltpu.HBM)
    return call(
        functools.partial(down_kernel, path, len(stages)),
        "down",
        2 * classes * rank * (sum(path) * rank + leaves * size * 2),
        rank * rank,
        8 * 2**20,
        vmem=24,
        out_shape=pltpu.HBM(own.shape, F32),
        in_specs=[pl.BlockSpec(memory_space=pltpu.SMEM)] + [hbm] * len(inputs),
        out_specs=pl.BlockSpec(memory_space=pltpu.VMEM),
        scratch_shapes=[
            pltpu.VMEM(lifted.shape, BF16),
            pltpu.VMEM(terms.shape, F32),
            pltpu.VMEM(up.shape, BF16),
            pltpu.VMEM((sum(path), rank, rank), BF16),
            pltpu.VMEM((sum(path), classes, rank), F32),
            pltpu.VMEM((2 * leaves, classes, rank), BF16),
            pltpu.SemaphoreType.DMA((sum(path), 2)),
            pltpu.SemaphoreType.DMA((leaves,)),
            pltpu.SemaphoreType.DMA((3,)),
        ],
    )(in_hbm(numbers), *(in_hbm(array) for array in inputs))


def near_kernel(
    rows, group, resident, slots, halves_ref, targets_hbm, start_hbm, block_hbm, out_ref, *refs
):
    order, leaf_state, block_state, targets_ref, start_ref = refs[:5]
    leaf_sems, block_sems, start_sem = refs[-3:]
    block_ref = block_hbm if resident else refs[5]
    leaves, width, size = targets_ref.shape
    sources = block_hbm.shape[0]
    classes = out_ref.shape[0]
    inverse_leaf = 1.0 / math.sqrt(size)

    def target_copy(leaf):
        return pltpu.make_async_copy(
            targets_hbm.at[leaf], targets_ref.at[leaf], leaf_sems.at[leaf]
        )

    def block_copy(source):
        return pltpu.make_async_copy(
            block_hbm.at[source], block_ref.at[source], block_sems.at[source]
        )

    def clear(source, carry):
        block_state[source] = 0
        return carry

    def list_leaf(number, filled):
        target_copy(number).start()
        leaf_state[number] = 1

        def list_slot(slot, carry):
            source = lax.rem(slots[number, slot] // leaves, sources)
            place = filled + (slot - 1) // 2

            @pl.when(lax.rem(slot, 2) == 1)
            def _():
                order[place, 0] = number
                order[place, 1] = source
                order[place, 2] = source
                order[place, 3] = 0

            @pl.when(lax.rem(slot, 2) == 0)
            def _():
                order[place, 2] = source
                order[place, 3] = 1

            if not resident:

                @pl.when(block_state[source] == 0)
                def _():
                    block_state[source] = 1
                    block_copy(source).start()

            return carry

        live = slots[number, slots.shape[1] - 1]
        lax.fori_loop(1, live, list_slot, 0)
        return filled + live // 2

    def repeat_last(number, carry):
        for field in range(4):
            order[number, field] = order[count - 1, field]
        return carry

    if not resident:
        lax.fori_loop(0, sources, clear, 0)
    count = lax.fori_loop(0, leaves, list_leaf, 0)
    start_copy = pltpu.make_async_copy(start_hbm, start_ref, start_sem)
    start_copy.start()
    steps = (count + group - 1) // group
    lax.fori_loop(count, steps * group, repeat_last, 0)
    out_ref[...] = jnp.zeros_like(out_ref)

    def arrive(number):
        leaf = order[number, 0]

        @pl.when(leaf_state[leaf] == 1)
        def _():
            leaf_state[leaf] = 2
            target_copy(leaf).wait()

        for field in (1, 2) if not resident else ():
            source = order[number, field]

            @pl.when(block_state[source] == 1)
            def _():
                block_state[source] = 2
                block_copy(source).wait()

    def scores_of(source):
        found = []
        for column in range(0, rows, width):
            columns = min(width, rows - column)
            place = pl.ds(rows + column * classes // width, classes * columns // width)
            weights = block_ref[source, place, :]
            if columns < width:
                weights = jnp.concatenate(
                    [weights[:, : width // 2], weights[:, width // 2 :]], axis=0
                )
            found.append(weights)
        return found

    def contribution(number):
        leaf, one, two = order[number, 0], order[number, 1], order[number, 2]
        block = jnp.concatenate(
            [block_ref[one, pl.ds(0, rows), :], block_ref[two, pl.ds(0, rows), :]], axis=0
        )
        inner = dot(block, targets_ref[leaf])
        tile = kappa_of(inner, width, half_exponents(block), halves_ref[leaf]).astype(BF16)
        second = order[number, 3].astype(F32)
        scores = scores_of(one)
        scores += [(part.astype(F32) * second).astype(BF16) for part in scores_of(two)]
        added = dot(jnp.concatenate(scores, axis=1), tile)
        return added * jnp.where(number < count, inverse_leaf, 0.0)

    def step(first, carry):
        numbers = [first * group + k for k in range(group)]
        for number in numbers:
            arrive(number)
        added = [contribution(number) for number in numbers]
        for number, term in zip(numbers, added):
            columns = pl.ds(pl.multiple_of(order[number, 0] * size, size), size)
            out_ref[:, columns] += term
        return carry

    lax.fori_loop(0, steps, step, 0)
    start_copy.wait()
    out_ref[...] += start_ref[...]


def near_part(rows, group, slots, targets, halves, start, blocks, resident, out_type):
    classes, columns = start.shape
    leaves, width, size = targets.shape
    tiles = 24
    whole = pl.BlockSpec(memory_space=pltpu.VMEM)
    hbm = pl.BlockSpec(memory_space=pltpu.HBM)
    scratch = [
        pltpu.SMEM((slots.size // 2 + group, 4), jnp.int32),
        pltpu.SMEM((leaves,), jnp.int32),
        pltpu.SMEM((blocks.shape[0],), jnp.int32),
        pltpu.VMEM(targets.shape, BF16),
        pltpu.VMEM(start.shape, F32),
    ]
    if not resident:
        scratch.append(pltpu.VMEM(blocks.shape, BF16))
    scratch += [
        pltpu.SemaphoreType.DMA((leaves,)),
        pltpu.SemaphoreType.DMA((blocks.shape[0],)),
        pltpu.SemaphoreType.DMA,
    ]
    return call(
        functools.partial(near_kernel, rows, group, resident),
        "near",
        tiles * 2 * rows * size * (width + classes),
        tiles * rows * size,
        tiles * rows * width * 2 + 4 * 2**20,
        vmem=24,
        out_shape=out_type(start.shape, F32),
        in_specs=[
            pl.BlockSpec(memory_space=pltpu.SMEM),
            whole,
            hbm,
            hbm,
            whole if resident else hbm,
        ],
        out_specs=whole,
        scratch_shapes=scratch,
    )(
        in_hbm(slots),
        in_hbm(halves),
        in_hbm(targets),
        in_hbm(start),
        blocks if resident else in_hbm(blocks),
    )


def swap(value, axis, mask):
    pairs = [(source, source ^ mask) for source in range(lax.axis_size(axis))]
    return lax.ppermute(value, axis, pairs)


def per_device(points, weights, near, counts, skel_leaf, skel_local, skel_upper):
    leaves, rank = skel_leaf.shape
    size = points.shape[0] // leaves
    classes = weights.shape[0]
    slots = near.shape[1]
    sub_count = lax.axis_size("sub")
    grp_count = lax.axis_size("grp")
    sub_index = lax.axis_index("sub")
    grp_index = lax.axis_index("grp")
    device = grp_index * sub_count + sub_index

    group_first = grp_index * sub_count * leaves
    slot_ids = jnp.arange(slots)
    group_rows = lax.dynamic_slice_in_dim(near, group_first, sub_count * leaves, 0)
    group_counts = lax.dynamic_slice_in_dim(counts, group_first, sub_count * leaves, 0)
    owned = (
        (group_rows // leaves == device)
        & (slot_ids[None, :] < group_counts[:, None])
        & (slot_ids[None, :] > 0)
    )
    chosen = jnp.where(owned, group_rows - device * leaves, -1).reshape(sub_count, leaves * slots)
    chosen = jnp.max(chosen, axis=1)

    first_rows = size - LAST_ROWS
    sent = pack(chosen, points, weights, size, 0, first_rows)
    arrived = lax.all_to_all(sent, "sub", split_axis=0, concat_axis=0, tiled=True)

    sub_bits = sub_count.bit_length() - 1
    far_bits = (sub_bits - 1) // 2
    steps = [1, sub_bits - 1 - far_bits, far_bits, grp_count.bit_length() - 1]
    table, starts, path_lengths = place_table(steps)
    mine = lax.dynamic_slice_in_dim(jnp.asarray(table), device, 1, 0)[0]
    *stage_rows, path_nodes = (mine[low:high] for low, high in zip(starts[:-1], starts[1:]))
    near_slots = jnp.concatenate(
        [
            lax.dynamic_slice_in_dim(near, device * leaves, leaves, 0),
            lax.dynamic_slice_in_dim(counts, device * leaves, leaves, 0)[:, None],
        ],
        axis=1,
    )

    own, skel, up, summary, targets, halves = leaf_level(points, weights, skel_leaf)
    lifted, terms, state = subtree(
        "local",
        leaves,
        leaves - 1,
        0,
        jnp.arange(leaves, dtype=jnp.int32),
        skel_local,
        (skel, summary),
        classes,
    )
    state, near_slots, stage_rows, path_nodes = lax.optimization_barrier(
        (state, near_slots, stage_rows, path_nodes)
    )

    def exchange(state, stage):
        axis = "grp" if stage + 1 == len(steps) else "sub"
        low = 0 if axis == "grp" else sum(steps[:stage])
        return [state] + [swap(state, axis, mask << low) for mask in range(1, 1 << steps[stage])]

    def climb(name, states, stage, rows):
        count = 1 << steps[stage]
        inner = count - 2 if stage + 1 == len(steps) else count - 1
        *done, state = subtree(name, count, inner, 2, rows, skel_upper, states, classes)
        return done, state

    core_stage, state = climb("core_nodes", exchange(state, 0), 0, stage_rows[0])
    x_states = exchange(state, 1)
    sent_last = pack(chosen, points, weights, size, first_rows, LAST_ROWS)
    sent_last, x_rows = lax.optimization_barrier((sent_last, stage_rows[1]))
    x_stage, state = climb("x_nodes", x_states, 1, x_rows)
    y_states = exchange(state, 2)
    sent_last, _ = lax.optimization_barrier((sent_last, y_states))
    arrived_last = lax.all_to_all(sent_last, "sub", split_axis=0, concat_axis=0, tiled=True)

    y_stage, state = climb("y_nodes", y_states, 2, stage_rows[2])
    z_states = exchange(state, 3)
    near_slots, _ = lax.optimization_barrier((near_slots, state))
    total = near_part(
        first_rows, GROUP, near_slots, targets, halves, own, arrived, False, pltpu.HBM
    )
    z_rows, total = lax.optimization_barrier((stage_rows[3], total))
    z_stage, _ = climb("z_nodes", z_states, 3, z_rows)
    stages = [z_stage, y_stage, x_stage, core_stage]
    total = down(path_nodes, path_lengths, stages, lifted, terms, up, total)
    return near_part(
        LAST_ROWS,
        GROUP,
        near_slots,
        targets,
        halves,
        total,
        arrived_last,
        False,
        jax.ShapeDtypeStruct,
    )


def solution(mesh):
    split = P(("grp", "sub"), None)
    columns = P(None, ("grp", "sub"))
    return jax.shard_map(
        per_device,
        mesh=mesh,
        in_specs=(split, columns, P(), P(), split, split, P()),
        out_specs=columns,
        check_vma=False,
    )
```

profile of v0, /device:TPU:96, one launch (start us, length us, event | category | flops | bytes accessed | tf_op | source)
XLA Modules:
  0.0 180.3 jit_solution(8626719962221885036)
XLA Ops:
  1.8 4.5 %pack.3 = bf16[32,320,256]{2,1,0:T(8,128)(2,1)} custom-call(s32[32]{0:T(128)S(1)} %reduce_max.18.chosen, bf16[4096,256]{1,0:T(8,128)(2,1)} %points_ref.5, bf16[64,4096]{1,0:T(8,128)(2,1)} %weights_ref.5), custom_call_target="tpu_custom_call" | custom-call | bytes 10485760 | tf_op jit(solution)/shard_map/pack/pallas_call | solution.py:135
  6.3 7.4 %all-to-all-start = ((bf16[32,320,256]{2,1,0:T(8,128)(2,1)}), bf16[32,320,256]{2,1,0:T(8,128)(2,1)}, u32[]{:S(2)}, u32[]{:S(2)}) async-start(bf16[32,320,256]{2,1,0:T(8,128)(2,1)} %pack.3), calls=%async_computation | async-start | bytes 10485760 | tf_op jit(solution)/shard_map/all_to_all | solution.py:644
  16.8 8.8 %leaf.1 = (f32[64,4096]{1,0:T(8,128)}, bf16[8,256,256]{2,1,0:T(8,128)(2,1)S(1)}, bf16[8,512,256]{2,1,0:T(8,128)(2,1)}, bf16[8,64,256]{2,1,0:T(8,128)(2,1)S(1)}, ...) custom-call(bf16[4096,256]{1,0:T(8,128)(2,1)S(1)} %copy-done, bf16[64,4096]{1,0:T(8,128)(2,1)S(1)} %copy-done.1, ...), custom_call_target="tpu_custom_call" | custom-call | flops 3087007744 | bytes 8388608 | tf_op jit(solution)/shard_map/leaf/pallas_call | solution.py:197
  26.1 9.3 %local.1 = (bf16[7,512,256]{2,1,0:T(8,128)(2,1)}, f32[14,64,256]{2,1,0:T(8,128)}, bf16[320,256]{1,0:T(8,128)(2,1)S(1)}) custom-call(s32[8]{0:T(128)} %iota.10.rows, s32[7,256]{1,0:T(8,128)} %refs_0_.5, bf16[8,256,256]{2,1,0:T(8,128)(2,1)S(1)} %get-tuple-element.38.refs_1_, bf16[8,64,256]{2,1,0:T(8,128)(2,1)S(1)} %get-tuple-element.39.refs_2_), custom_call_target="tpu_custom_call" | custom-call | flops 1409286144 | bytes 6291456 | tf_op jit(solution)/shard_map/local/pallas_call | solution.py:289
  38.1 1.2 collective-permute-done.refs_2_
  39.3 3.1 %core_nodes.1 = (bf16[1,512,256]{2,1,0:T(8,128)(2,1)}, f32[2,64,256]{2,1,0:T(8,128)}, bf16[320,256]{1,0:T(8,128)(2,1)S(1)}) custom-call(s32[2]{0:T(128)} %slice_bitcast_fusion.4.rows, s32[126,256]{1,0:T(8,128)} %refs_0_.9, bf16[320,256]{1,0:T(8,128)(2,1)S(1)} %get-tuple-element.46.refs_1_, bf16[320,256]{1,0:T(8,128)(2,1)S(1)} %collective-permute-done.refs_2_), custom_call_target="tpu_custom_call" | custom-call | flops 201326592 | bytes 6291456 | tf_op jit(solution)/shard_map/core_nodes/pallas_call | solution.py:289
  42.4 2.9 %collective-permute-start.3 = (bf16[320,256]{1,0:T(8,128)(2,1)S(1)}, bf16[320,256]{1,0:T(8,128)(2,1)S(1)}, u32[]{:S(2)}, u32[]{:S(2)}) collective-permute-start(bf16[320,256]{1,0:T(8,128)(2,1)S(1)} %get-tuple-element.47.refs_1_), channel_id=1, source_target_pairs={{0,6},{1,7},{2,4},{3,5},{4,2},{5,3},{6,0},{7,1},{8,14},{9,15},{10,... | collective-permute-start | bytes 491528 | tf_op jit(solution)/shard_map/ppermute | solution.py:616
  45.3 0.9 collective-permute-start.2
  46.5 4.5 %pack.2 = bf16[32,320,256]{2,1,0:T(8,128)(2,1)} custom-call(s32[32]{0:T(128)S(1)} %reduce_max.18.chosen, bf16[4096,256]{1,0:T(8,128)(2,1)} %points_ref.5, bf16[64,4096]{1,0:T(8,128)(2,1)} %weights_ref.5), custom_call_target="tpu_custom_call" | custom-call | bytes 10485760 | tf_op jit(solution)/shard_map/pack/pallas_call | solution.py:135
  50.9 31.1 %collective-permute-done.3.refs_4_ = bf16[320,256]{1,0:T(8,128)(2,1)S(1)} collective-permute-done((bf16[320,256]{1,0:T(8,128)(2,1)S(1)}, bf16[320,256]{1,0:T(8,128)(2,1)S(1)}, u32[]{:S(2)}, u32[]{:S(2)}) %collective-permute-start.3) | collective-permute-done | bytes 163872 | tf_op jit(solution)/shard_map/ppermute | solution.py:616
  82.8 5.2 %x_nodes.1 = (bf16[3,512,256]{2,1,0:T(8,128)(2,1)}, f32[6,64,256]{2,1,0:T(8,128)}, bf16[320,256]{1,0:T(8,128)(2,1)S(1)}) custom-call(s32[4]{0:T(128)} %get-tuple-element.44.rows, s32[126,256]{1,0:T(8,128)} %refs_0_.9, bf16[320,256]{1,0:T(8,128)(2,1)S(1)} %get-tuple-element.47.refs_1_, bf16[320,256]{1,0:T(8,128)(2,1)S(1)} %collective-permute-done.1.refs_2_, ...), custom_call_target="tpu_custom_call" | custom-call | flops 603979776 | bytes 6291456 | tf_op jit(solution)/shard_map/x_nodes/pallas_call | solution.py:289
  88.1 1.5 collective-permute-start.6
  89.6 1.3 collective-permute-start.5
  90.9 1.3 collective-permute-start.4
  92.2 6.4 %collective-permute-done.6.refs_4_ = bf16[320,256]{1,0:T(8,128)(2,1)S(1)} collective-permute-done((bf16[320,256]{1,0:T(8,128)(2,1)S(1)}, bf16[320,256]{1,0:T(8,128)(2,1)S(1)}, u32[]{:S(2)}, u32[]{:S(2)}) %collective-permute-start.6) | collective-permute-done | bytes 163872 | tf_op jit(solution)/shard_map/ppermute | solution.py:616
  99.2 6.7 %all-to-all-start.1 = ((bf16[32,320,256]{2,1,0:T(8,128)(2,1)}), bf16[32,320,256]{2,1,0:T(8,128)(2,1)}, u32[]{:S(2)}, u32[]{:S(2)}) async-start(bf16[32,320,256]{2,1,0:T(8,128)(2,1)} %pack.2), calls=%async_computation.1 | async-start | bytes 10485760 | tf_op jit(solution)/shard_map/all_to_all | solution.py:693
  105.9 5.2 %y_nodes.1 = (bf16[3,512,256]{2,1,0:T(8,128)(2,1)}, f32[6,64,256]{2,1,0:T(8,128)}, bf16[320,256]{1,0:T(8,128)(2,1)S(1)}) custom-call(s32[4]{0:T(128)} %get-tuple-element.42.rows, s32[126,256]{1,0:T(8,128)} %refs_0_.9, bf16[320,256]{1,0:T(8,128)(2,1)S(1)} %get-tuple-element.48.refs_1_, bf16[320,256]{1,0:T(8,128)(2,1)S(1)} %collective-permute-done.4.refs_2_, ...), custom_call_target="tpu_custom_call" | custom-call | flops 603979776 | bytes 6291456 | tf_op jit(solution)/shard_map/y_nodes/pallas_call | solution.py:289
  111.1 2.5 %collective-permute-start.8 = (bf16[320,256]{1,0:T(8,128)(2,1)S(1)}, bf16[320,256]{1,0:T(8,128)(2,1)S(1)}, u32[]{:S(2)}, u32[]{:S(2)}) collective-permute-start(bf16[320,256]{1,0:T(8,128)(2,1)S(1)} %get-tuple-element.49.refs_1_), channel_id=1, source_target_pairs={{0,64},{32,96},{64,0},{96,32},{1,65},{33,97},{65,1},{97,33},{2,66}... | collective-permute-start | bytes 491528 | tf_op jit(solution)/shard_map/ppermute | solution.py:616
  113.6 1.6 collective-permute-start.7
  115.2 8.7 %near.2.refs_11_ = f32[64,4096]{1,0:T(8,128)} custom-call(s32[8,9]{1,0:T(8,128)} %pad_add_fusion.slots, f32[8,1,512]{2,1,0:T(1,128)} %get-tuple-element.51.halves_ref, bf16[8,256,512]{2,1,0:T(8,128)(2,1)} %get-tuple-element.52.targets_hbm, f32[64,4096]{1,0:T(8,128)} %get-tuple-element.55.start_hbm, bf16[32,320,256]{2,1,0:T(8,128)(2,1)} %all-to-all-done.block_hbm), custom_call_target="tpu_custom_call" | custom-call | flops 2013265920 | bytes 7340032 | tf_op jit(solution)/shard_map/near/pallas_call | solution.py:588
  123.9 4.8 %z_nodes.1 = (bf16[2,512,256]{2,1,0:T(8,128)(2,1)}, f32[6,64,256]{2,1,0:T(8,128)}, bf16[320,256]{1,0:T(8,128)(2,1)}) custom-call(s32[3]{0:T(128)} %slice_bitcast_fusion.1.rows, s32[126,256]{1,0:T(8,128)} %refs_0_.9, bf16[320,256]{1,0:T(8,128)(2,1)S(1)} %get-tuple-element.49.refs_1_, bf16[320,256]{1,0:T(8,128)(2,1)S(1)} %collective-permute-done.7.refs_2_, ...), custom_call_target="tpu_custom_call" | custom-call | flops 402653184 | bytes 6291456 | tf_op jit(solution)/shard_map/z_nodes/pallas_call | solution.py:289
  128.7 8.0 %down.1.start_hbm = f32[64,4096]{1,0:T(8,128)} custom-call(s32[7]{0:T(128)} %slice_bitcast_fusion.numbers, bf16[2,512,256]{2,1,0:T(8,128)(2,1)} %get-tuple-element.57.refs_0_, f32[6,64,256]{2,1,0:T(8,128)} %get-tuple-element.58.refs_1_, bf16[3,512,256]{2,1,0:T(8,128)(2,1)} %get-tuple-element.59.refs_2_, f32[6,64,256]{2,1,0:T(8,128)} %get-tuple-element.60.refs_3_, ...), custom_call_target="tpu_custom_call" | custom-call | flops 327155712 | bytes 8388608 | tf_op jit(solution)/shard_map/down/pallas_call | solution.py:415
  136.8 34.9 %all-to-all-done.1.block_hbm = bf16[32,320,256]{2,1,0:T(8,128)(2,1)} async-done(((bf16[32,320,256]{2,1,0:T(8,128)(2,1)}), bf16[32,320,256]{2,1,0:T(8,128)(2,1)}, u32[]{:S(2)}, u32[]{:S(2)}) %all-to-all-start.1) | async-done | bytes 5242912 | tf_op jit(solution)/shard_map/all_to_all | solution.py:693
  171.6 8.7 %near.3 = f32[64,4096]{1,0:T(8,128)} custom-call(s32[8,9]{1,0:T(8,128)} %pad_add_fusion.slots, f32[8,1,512]{2,1,0:T(1,128)} %get-tuple-element.51.halves_ref, bf16[8,256,512]{2,1,0:T(8,128)(2,1)} %get-tuple-element.52.targets_hbm, f32[64,4096]{1,0:T(8,128)} %down.1.start_hbm, bf16[32,320,256]{2,1,0:T(8,128)(2,1)} %all-to-all-done.1.block_hbm), custom_call_target="tpu_custom_call" | custom-call | flops 2013265920 | bytes 7340032 | tf_op jit(solution)/shard_map/near/pallas_call | solution.py:588
  (33 shorter events, 9.8 us)
Async XLA Ops:
  6.3 10.5 %copy-start = (bf16[4096,256]{1,0:T(8,128)(2,1)S(1)}, bf16[4096,256]{1,0:T(8,128)(2,1)}, u32[]{:S(2)}) copy-start(bf16[4096,256]{1,0:T(8,128)(2,1)} %points_ref.5) | copy-start | bytes 6291460
  6.3 10.5 %copy-start.1 = (bf16[64,4096]{1,0:T(8,128)(2,1)S(1)}, bf16[64,4096]{1,0:T(8,128)(2,1)}, u32[]{:S(2)}) copy-start(bf16[64,4096]{1,0:T(8,128)(2,1)} %weights_ref.5) | copy-start | bytes 1572868
  6.3 10.5 %copy-start.2 = (s32[8,256]{1,0:T(8,128)S(1)}, s32[8,256]{1,0:T(8,128)}, u32[]{:S(2)}) copy-start(s32[8,256]{1,0:T(8,128)} %chosen_ref.1) | copy-start | bytes 24580
  6.3 92.8 %all-to-all-start = ((bf16[32,320,256]{2,1,0:T(8,128)(2,1)}), bf16[32,320,256]{2,1,0:T(8,128)(2,1)}, u32[]{:S(2)}, u32[]{:S(2)}) async-start(bf16[32,320,256]{2,1,0:T(8,128)(2,1)} %pack.3), calls=%async_computation | async-start | bytes 10485760 | tf_op jit(solution)/shard_map/all_to_all | solution.py:644
  37.9 1.4 collective-permute-start
  42.4 39.6 %collective-permute-start.3 = (bf16[320,256]{1,0:T(8,128)(2,1)S(1)}, bf16[320,256]{1,0:T(8,128)(2,1)S(1)}, u32[]{:S(2)}, u32[]{:S(2)}) collective-permute-start(bf16[320,256]{1,0:T(8,128)(2,1)S(1)} %get-tuple-element.47.refs_1_), channel_id=1, source_target_pairs={{0,6},{1,7},{2,4},{3,5},{4,2},{5,3},{6,0},{7,1},{8,14},{9,15},{10,... | collective-permute-start | bytes 491528 | tf_op jit(solution)/shard_map/ppermute | solution.py:616
  45.3 36.7 %collective-permute-start.2 = (bf16[320,256]{1,0:T(8,128)(2,1)S(1)}, bf16[320,256]{1,0:T(8,128)(2,1)S(1)}, u32[]{:S(2)}, u32[]{:S(2)}) collective-permute-start(bf16[320,256]{1,0:T(8,128)(2,1)S(1)} %get-tuple-element.47.refs_1_), channel_id=1, source_target_pairs={{0,4},{1,5},{2,6},{3,7},{4,0},{5,1},{6,2},{7,3},{8,12},{9,13},{10,... | collective-permute-start | bytes 491528 | tf_op jit(solution)/shard_map/ppermute | solution.py:616
  46.2 36.6 %collective-permute-start.1 = (bf16[320,256]{1,0:T(8,128)(2,1)S(1)}, bf16[320,256]{1,0:T(8,128)(2,1)S(1)}, u32[]{:S(2)}, u32[]{:S(2)}) collective-permute-start(bf16[320,256]{1,0:T(8,128)(2,1)S(1)} %get-tuple-element.47.refs_1_), channel_id=1, source_target_pairs={{0,2},{1,3},{2,0},{3,1},{4,6},{5,7},{6,4},{7,5},{8,10},{9,11},{10,... | collective-permute-start | bytes 491528 | tf_op jit(solution)/shard_map/ppermute | solution.py:616
  88.1 10.5 %collective-permute-start.6 = (bf16[320,256]{1,0:T(8,128)(2,1)S(1)}, bf16[320,256]{1,0:T(8,128)(2,1)S(1)}, u32[]{:S(2)}, u32[]{:S(2)}) collective-permute-start(bf16[320,256]{1,0:T(8,128)(2,1)S(1)} %get-tuple-element.48.refs_1_), channel_id=1, source_target_pairs={{0,24},{1,25},{2,26},{3,27},{4,28},{5,29},{6,30},{7,31},{8,16},{9,... | collective-permute-start | bytes 491528 | tf_op jit(solution)/shard_map/ppermute | solution.py:616
  89.6 8.9 %collective-permute-start.5 = (bf16[320,256]{1,0:T(8,128)(2,1)S(1)}, bf16[320,256]{1,0:T(8,128)(2,1)S(1)}, u32[]{:S(2)}, u32[]{:S(2)}) collective-permute-start(bf16[320,256]{1,0:T(8,128)(2,1)S(1)} %get-tuple-element.48.refs_1_), channel_id=1, source_target_pairs={{0,16},{1,17},{2,18},{3,19},{4,20},{5,21},{6,22},{7,23},{8,24},{9,... | collective-permute-start | bytes 491528 | tf_op jit(solution)/shard_map/ppermute | solution.py:616
  90.9 8.3 %collective-permute-start.4 = (bf16[320,256]{1,0:T(8,128)(2,1)S(1)}, bf16[320,256]{1,0:T(8,128)(2,1)S(1)}, u32[]{:S(2)}, u32[]{:S(2)}) collective-permute-start(bf16[320,256]{1,0:T(8,128)(2,1)S(1)} %get-tuple-element.48.refs_1_), channel_id=1, source_target_pairs={{0,8},{1,9},{2,10},{3,11},{4,12},{5,13},{6,14},{7,15},{8,0},{9,1},... | collective-permute-start | bytes 491528 | tf_op jit(solution)/shard_map/ppermute | solution.py:616
  99.2 72.5 %all-to-all-start.1 = ((bf16[32,320,256]{2,1,0:T(8,128)(2,1)}), bf16[32,320,256]{2,1,0:T(8,128)(2,1)}, u32[]{:S(2)}, u32[]{:S(2)}) async-start(bf16[32,320,256]{2,1,0:T(8,128)(2,1)} %pack.2), calls=%async_computation.1 | async-start | bytes 10485760 | tf_op jit(solution)/shard_map/all_to_all | solution.py:693
  111.1 12.8 %collective-permute-start.9 = (bf16[320,256]{1,0:T(8,128)(2,1)S(1)}, bf16[320,256]{1,0:T(8,128)(2,1)S(1)}, u32[]{:S(2)}, u32[]{:S(2)}) collective-permute-start(bf16[320,256]{1,0:T(8,128)(2,1)S(1)} %get-tuple-element.49.refs_1_), channel_id=1, source_target_pairs={{0,96},{32,64},{64,32},{96,0},{1,97},{33,65},{65,33},{97,1},{2,98}... | collective-permute-start | bytes 491528 | tf_op jit(solution)/shard_map/ppermute | solution.py:616
  111.1 12.8 %collective-permute-start.8 = (bf16[320,256]{1,0:T(8,128)(2,1)S(1)}, bf16[320,256]{1,0:T(8,128)(2,1)S(1)}, u32[]{:S(2)}, u32[]{:S(2)}) collective-permute-start(bf16[320,256]{1,0:T(8,128)(2,1)S(1)} %get-tuple-element.49.refs_1_), channel_id=1, source_target_pairs={{0,64},{32,96},{64,0},{96,32},{1,65},{33,97},{65,1},{97,33},{2,66}... | collective-permute-start | bytes 491528 | tf_op jit(solution)/shard_map/ppermute | solution.py:616
  113.6 10.3 %collective-permute-start.7 = (bf16[320,256]{1,0:T(8,128)(2,1)S(1)}, bf16[320,256]{1,0:T(8,128)(2,1)S(1)}, u32[]{:S(2)}, u32[]{:S(2)}) collective-permute-start(bf16[320,256]{1,0:T(8,128)(2,1)S(1)} %get-tuple-element.49.refs_1_), channel_id=1, source_target_pairs={{0,32},{32,0},{64,96},{96,64},{1,33},{33,1},{65,97},{97,65},{2,34}... | collective-permute-start | bytes 491528 | tf_op jit(solution)/shard_map/ppermute | solution.py:616
where the time goes:
time: 183 us; the launch traced here: 180 us
  waiting for transfers between devices  74.9 us (41%)
  Pallas kernels  70.8 us (39%)
  starting transfers between devices  26.6 us (15%)
  local copies, waits for them, and re-layouts  6.25 us (3%)
    ppermute x10, waiting for transfers between devices, swap(): return lax.ppermute(value, axis, pairs)  40.1 us
    all_to_all x1, waiting for transfers between devices, per_device(): lax.all_to_all(sent_last, 'sub', split_axis=0, concat_axis=0, tiled=True)  34.9 us
    pallas_call x5, Pallas kernels, subtree(): call(functools.partial(subtree_kernel, count, inner, states), name, inner...  27.7 us
    pallas_call x2, Pallas kernels, near_part(): call(functools.partial(near_kernel, rows, group, resident), 'near', tiles...  17.4 us
    ppermute x10, starting transfers between devices, swap(): return lax.ppermute(value, axis, pairs)  12.5 us
    pallas_call x2, Pallas kernels, pack(): call(functools.partial(pack_kernel, leaf_size, first, rows), 'pack', 0, 0...  8.96 us
    pallas_call x1, Pallas kernels, leaf_level(): call(leaf_kernel, 'leaf', leaves * 2 * size * (size * (width + classes +...  8.76 us
    pallas_call x1, Pallas kernels, down(): call(functools.partial(down_kernel, path, len(stages)), 'down', 2 * class...  8.04 us
  transfers between devices with their start and end apart: 12, of which 6 were waited for; matrix products, arithmetic and copies ran while one was open for 3% of the time, Pallas kernels for 32%

commit v1 on v0

--- a/solution.py
+++ b/solution.py
@@ -13,7 +13,7 @@
 BF16 = jnp.bfloat16
 LOG2E = 1.4426950408889634
 NT = (((1,), (1,)), ((), ()))
-LAST_ROWS = 256
+PARTS = (256, 128, 128)
 GROUP = 1
 
 
@@ -263,7 +263,11 @@
         pair(i, even, odd, half[:rank], half[rank:])
         return carry
 
-    lax.fori_loop(0, inner, step, 0)
+    if count > 4:
+        lax.fori_loop(0, inner, step, 0)
+    else:
+        for i in range(inner):
+            step(i, 0)
     if inner == count - 1:
         state_ref[pl.ds(0, rank), :] = nodes[count + inner - 1]
         state_ref[pl.ds(rank, classes), :] = sums[count + inner - 1]
@@ -392,14 +396,10 @@
     for copy in local_copies:
         copy.wait()
 
-    def lower(step, carry):
-        i = inner - 1 - step
-        down = dot_nt(values[leaves + i], lifted_ref[i]) * inverse_rank
-        values[2 * i] = (terms_ref[2 * i] + down[:, :rank]).astype(BF16)
-        values[2 * i + 1] = (terms_ref[2 * i + 1] + down[:, rank:]).astype(BF16)
-        return carry
-
-    lax.fori_loop(0, inner, lower, 0)
+    for i in range(inner - 1, -1, -1):
+        below = dot_nt(values[leaves + i], lifted_ref[i]) * inverse_rank
+        values[2 * i] = (terms_ref[2 * i] + below[:, :rank]).astype(BF16)
+        values[2 * i + 1] = (terms_ref[2 * i + 1] + below[:, rank:]).astype(BF16)
     own_copy.wait()
     for leaf in range(leaves):
         up_copies[leaf].wait()
@@ -639,9 +639,10 @@
     chosen = jnp.where(owned, group_rows - device * leaves, -1).reshape(sub_count, leaves * slots)
     chosen = jnp.max(chosen, axis=1)
 
-    first_rows = size - LAST_ROWS
-    sent = pack(chosen, points, weights, size, 0, first_rows)
-    arrived = lax.all_to_all(sent, "sub", split_axis=0, concat_axis=0, tiled=True)
+    def send(block):
+        return lax.all_to_all(block, "sub", split_axis=0, concat_axis=0, tiled=True)
+
+    arrived = [send(pack(chosen, points, weights, size, 0, PARTS[0]))]
 
     sub_bits = sub_count.bit_length() - 1
     far_bits = (sub_bits - 1) // 2
@@ -685,34 +686,32 @@
 
     core_stage, state = climb("core_nodes", exchange(state, 0), 0, stage_rows[0])
     x_states = exchange(state, 1)
-    sent_last = pack(chosen, points, weights, size, first_rows, LAST_ROWS)
-    sent_last, x_rows = lax.optimization_barrier((sent_last, stage_rows[1]))
+    sent = [
+        pack(chosen, points, weights, size, sum(PARTS[:part]), PARTS[part]) for part in (1, 2)
+    ]
+    sent, x_rows, x_states = lax.optimization_barrier((sent, stage_rows[1], x_states))
+    arrived.append(send(sent[0]))
     x_stage, state = climb("x_nodes", x_states, 1, x_rows)
     y_states = exchange(state, 2)
-    sent_last, _ = lax.optimization_barrier((sent_last, y_states))
-    arrived_last = lax.all_to_all(sent_last, "sub", split_axis=0, concat_axis=0, tiled=True)
-
+
+    def near_sum(part, slots, start, out_type=pltpu.HBM):
+        return near_part(
+            PARTS[part], GROUP, slots, targets, halves, start, arrived[part], part == 2, out_type
+        )
+
+    near_slots, _ = lax.optimization_barrier((near_slots, state))
+    total = near_sum(0, near_slots, own)
+    sent_last, _, _ = lax.optimization_barrier((sent[1], y_states, total))
+    arrived.append(send(sent_last))
     y_stage, state = climb("y_nodes", y_states, 2, stage_rows[2])
     z_states = exchange(state, 3)
     near_slots, _ = lax.optimization_barrier((near_slots, state))
-    total = near_part(
-        first_rows, GROUP, near_slots, targets, halves, own, arrived, False, pltpu.HBM
-    )
+    total = near_sum(1, near_slots, total)
     z_rows, total = lax.optimization_barrier((stage_rows[3], total))
     z_stage, _ = climb("z_nodes", z_states, 3, z_rows)
     stages = [z_stage, y_stage, x_stage, core_stage]
     total = down(path_nodes, path_lengths, stages, lifted, terms, up, total)
-    return near_part(
-        LAST_ROWS,
-        GROUP,
-        near_slots,
-        targets,
-        halves,
-        total,
-        arrived_last,
-        False,
-        jax.ShapeDtypeStruct,
-    )
+    return near_sum(2, near_slots, total, jax.ShapeDtypeStruct)
 
 
 def solution(mesh):

time: 183 us -> 183 us (level); the launches traced: 180 us -> 183 us
  waiting for transfers between devices: 74.9 us -> 45.8 us
  Pallas kernels: 70.8 us -> 96.8 us
  starting transfers between devices: 26.6 us -> 32.5 us
    all_to_all x2 -> x3, waiting for transfers between devices: 34.9 us -> 2.42 us  [send(): return lax.all_to_all(block, 'sub', split_axis=0, concat_axis=0, tiled=True)]
    pallas_call x2 -> x3, Pallas kernels: 17.4 us -> 42.3 us  [near_part(): call(functools.partial(near_kernel, rows, group, resident), 'near', tiles...]
    all_to_all x2 -> x3, starting transfers between devices: 14.1 us -> 20 us  [send(): return lax.all_to_all(block, 'sub', split_axis=0, concat_axis=0, tiled=True)]
    pallas_call x2 -> x3, Pallas kernels: 8.96 us -> 12.5 us  [pack(): call(functools.partial(pack_kernel, leaf_size, first, rows), 'pack', 0, 0...]
    ppermute x10, waiting for transfers between devices: 40.1 us -> 43.3 us  [swap(): return lax.ppermute(value, axis, pairs)]
  transfers between devices with their start and end apart: 12 -> 13, of which waited for: 6 -> 5; matrix products, arithmetic and copies ran while one was open for 3% -> 3% of each run, Pallas kernels for 32% -> 44%
where the time goes in v1:
time: 183 us
  Pallas kernels  96.8 us (53%)
  waiting for transfers between devices  45.8 us (25%)
  starting transfers between devices  32.5 us (18%)
  local copies, waits for them, and re-layouts  6.3 us (3%)
    ppermute x10, waiting for transfers between devices, swap(): return lax.ppermute(value, axis, pairs)  43.3 us
    pallas_call x3, Pallas kernels, near_part(): call(functools.partial(near_kernel, rows, group, resident), 'near', tiles...  42.3 us
    pallas_call x5, Pallas kernels, subtree(): call(functools.partial(subtree_kernel, count, inner, states), name, inner...  26 us
    all_to_all x3, starting transfers between devices, send(): return lax.all_to_all(block, 'sub', split_axis=0, concat_axis=0, tiled=True)  20 us
    ppermute x10, starting transfers between devices, swap(): return lax.ppermute(value, axis, pairs)  12.5 us
    pallas_call x3, Pallas kernels, pack(): call(functools.partial(pack_kernel, leaf_size, first, rows), 'pack', 0, 0...  12.5 us
    pallas_call x1, Pallas kernels, leaf_level(): call(leaf_kernel, 'leaf', leaves * 2 * size * (size * (width + classes +...  8.76 us
    pallas_call x1, Pallas kernels, down(): call(functools.partial(down_kernel, path, len(stages)), 'down', 2 * class...  7.26 us
  transfers between devices with their start and end apart: 13, of which 5 were waited for; matrix products, arithmetic and copies ran while one was open for 3% of the time, Pallas kernels for 44%

profile of v1, /device:TPU:96, one launch (start us, length us, event | category | flops | bytes accessed | tf_op | source)
XLA Modules:
  0.0 183.2 jit_solution(9957705071650824702)
XLA Ops:
  1.8 4.2 %pack.5 = bf16[32,320,256]{2,1,0:T(8,128)(2,1)} custom-call(s32[32]{0:T(128)S(1)} %reduce_max.18.chosen, bf16[4096,256]{1,0:T(8,128)(2,1)} %points_ref.7, bf16[64,4096]{1,0:T(8,128)(2,1)} %weights_ref.7), custom_call_target="tpu_custom_call" | custom-call | bytes 10485760 | tf_op jit(solution)/shard_map/pack/pallas_call | solution.py:135
  6.0 7.7 %all-to-all-start = ((bf16[32,320,256]{2,1,0:T(8,128)(2,1)}), bf16[32,320,256]{2,1,0:T(8,128)(2,1)}, u32[]{:S(2)}, u32[]{:S(2)}) async-start(bf16[32,320,256]{2,1,0:T(8,128)(2,1)} %pack.5), calls=%async_computation | async-start | bytes 10485760 | tf_op jit(solution)/shard_map/all_to_all | solution.py:643
  16.8 8.8 %leaf.1 = (f32[64,4096]{1,0:T(8,128)}, bf16[8,256,256]{2,1,0:T(8,128)(2,1)S(1)}, bf16[8,512,256]{2,1,0:T(8,128)(2,1)}, bf16[8,64,256]{2,1,0:T(8,128)(2,1)S(1)}, ...) custom-call(bf16[4096,256]{1,0:T(8,128)(2,1)S(1)} %copy-done, bf16[64,4096]{1,0:T(8,128)(2,1)S(1)} %copy-done.1, ...), custom_call_target="tpu_custom_call" | custom-call | flops 3087007744 | bytes 8388608 | tf_op jit(solution)/shard_map/leaf/pallas_call | solution.py:197
  26.1 9.4 %local.1 = (bf16[7,512,256]{2,1,0:T(8,128)(2,1)}, f32[14,64,256]{2,1,0:T(8,128)}, bf16[320,256]{1,0:T(8,128)(2,1)S(1)}) custom-call(s32[8]{0:T(128)} %iota.10.rows, s32[7,256]{1,0:T(8,128)} %refs_0_.5, bf16[8,256,256]{2,1,0:T(8,128)(2,1)S(1)} %get-tuple-element.44.refs_1_, bf16[8,64,256]{2,1,0:T(8,128)(2,1)S(1)} %get-tuple-element.45.refs_2_), custom_call_target="tpu_custom_call" | custom-call | flops 1409286144 | bytes 6291456 | tf_op jit(solution)/shard_map/local/pallas_call | solution.py:293
  38.3 1.2 collective-permute-done.refs_2_
  39.4 3.1 %core_nodes.1 = (bf16[1,512,256]{2,1,0:T(8,128)(2,1)}, f32[2,64,256]{2,1,0:T(8,128)}, bf16[320,256]{1,0:T(8,128)(2,1)S(1)}) custom-call(s32[2]{0:T(128)} %slice_bitcast_fusion.4.rows, s32[126,256]{1,0:T(8,128)} %refs_0_.9, bf16[320,256]{1,0:T(8,128)(2,1)S(1)} %get-tuple-element.50.refs_1_, bf16[320,256]{1,0:T(8,128)(2,1)S(1)} %collective-permute-done.refs_2_), custom_call_target="tpu_custom_call" | custom-call | flops 201326592 | bytes 6291456 | tf_op jit(solution)/shard_map/core_nodes/pallas_call | solution.py:293
  42.5 2.9 %collective-permute-start.3 = (bf16[320,256]{1,0:T(8,128)(2,1)S(1)}, bf16[320,256]{1,0:T(8,128)(2,1)S(1)}, u32[]{:S(2)}, u32[]{:S(2)}) collective-permute-start(bf16[320,256]{1,0:T(8,128)(2,1)S(1)} %get-tuple-element.53.refs_1_), channel_id=1, source_target_pairs={{0,6},{1,7},{2,4},{3,5},{4,2},{5,3},{6,0},{7,1},{8,14},{9,15},{10,... | collective-permute-start | bytes 491528 | tf_op jit(solution)/shard_map/ppermute | solution.py:616
  46.6 4.1 %pack.4 = bf16[32,160,256]{2,1,0:T(8,128)(2,1)} custom-call(s32[32]{0:T(128)S(1)} %reduce_max.18.chosen, bf16[4096,256]{1,0:T(8,128)(2,1)} %points_ref.7, bf16[64,4096]{1,0:T(8,128)(2,1)} %weights_ref.7), custom_call_target="tpu_custom_call" | custom-call | bytes 5242880 | tf_op jit(solution)/shard_map/pack/pallas_call | solution.py:135
  50.8 4.1 %pack.3 = bf16[32,160,256]{2,1,0:T(8,128)(2,1)} custom-call(s32[32]{0:T(128)S(1)} %reduce_max.18.chosen, bf16[4096,256]{1,0:T(8,128)(2,1)} %points_ref.7, bf16[64,4096]{1,0:T(8,128)(2,1)} %weights_ref.7), custom_call_target="tpu_custom_call" | custom-call | bytes 5242880 | tf_op jit(solution)/shard_map/pack/pallas_call | solution.py:135
  54.9 27.2 %collective-permute-done.3.refs_4_ = bf16[320,256]{1,0:T(8,128)(2,1)S(1)} collective-permute-done((bf16[320,256]{1,0:T(8,128)(2,1)S(1)}, bf16[320,256]{1,0:T(8,128)(2,1)S(1)}, u32[]{:S(2)}, u32[]{:S(2)}) %collective-permute-start.3) | collective-permute-done | bytes 163872 | tf_op jit(solution)/shard_map/ppermute | solution.py:616
  82.9 6.7 %all-to-all-start.1 = ((bf16[32,160,256]{2,1,0:T(8,128)(2,1)}), bf16[32,160,256]{2,1,0:T(8,128)(2,1)}, u32[]{:S(2)}, u32[]{:S(2)}) async-start(bf16[32,160,256]{2,1,0:T(8,128)(2,1)} %pack.3), calls=%async_computation.1 | async-start | bytes 5242880 | tf_op jit(solution)/shard_map/all_to_all | solution.py:643
  89.6 4.6 %x_nodes.1 = (bf16[3,512,256]{2,1,0:T(8,128)(2,1)}, f32[6,64,256]{2,1,0:T(8,128)}, bf16[320,256]{1,0:T(8,128)(2,1)S(1)}) custom-call(s32[4]{0:T(128)} %get-tuple-element.52.rows, s32[126,256]{1,0:T(8,128)} %refs_0_.9, bf16[320,256]{1,0:T(8,128)(2,1)S(1)} %get-tuple-element.53.refs_1_, bf16[320,256]{1,0:T(8,128)(2,1)S(1)} %collective-permute-done.1.refs_2_, ...), custom_call_target="tpu_custom_call" | custom-call | flops 603979776 | bytes 6291456 | tf_op jit(solution)/shard_map/x_nodes/pallas_call | solution.py:293
  94.2 3.0 %collective-permute-start.6 = (bf16[320,256]{1,0:T(8,128)(2,1)S(1)}, bf16[320,256]{1,0:T(8,128)(2,1)S(1)}, u32[]{:S(2)}, u32[]{:S(2)}) collective-permute-start(bf16[320,256]{1,0:T(8,128)(2,1)S(1)} %get-tuple-element.57.refs_1_), channel_id=1, source_target_pairs={{0,24},{1,25},{2,26},{3,27},{4,28},{5,29},{6,30},{7,31},{8,16},{9,... | collective-permute-start | bytes 491528 | tf_op jit(solution)/shard_map/ppermute | solution.py:616
  98.3 16.2 %near.3.start_hbm = f32[64,4096]{1,0:T(8,128)} custom-call(s32[8,9]{1,0:T(8,128)} %pad_add_fusion.slots, f32[8,1,512]{2,1,0:T(1,128)} %get-tuple-element.62.halves_ref, bf16[8,256,512]{2,1,0:T(8,128)(2,1)} %get-tuple-element.63.targets_hbm, f32[64,4096]{1,0:T(8,128)} %get-tuple-element.66.start_hbm, bf16[32,320,256]{2,1,0:T(8,128)(2,1)} %all-to-all-done.block_hbm), custom_call_target="tpu_custom_call" | custom-call | flops 2013265920 | bytes 7340032 | tf_op jit(solution)/shard_map/near/pallas_call | solution.py:588
  114.6 14.2 %collective-permute-done.6.refs_4_ = bf16[320,256]{1,0:T(8,128)(2,1)S(1)} collective-permute-done((bf16[320,256]{1,0:T(8,128)(2,1)S(1)}, bf16[320,256]{1,0:T(8,128)(2,1)S(1)}, u32[]{:S(2)}, u32[]{:S(2)}) %collective-permute-start.6) | collective-permute-done | bytes 163872 | tf_op jit(solution)/shard_map/ppermute | solution.py:616
  128.7 5.6 %all-to-all-start.2 = ((bf16[32,160,256]{2,1,0:T(8,128)(2,1)}), bf16[32,160,256]{2,1,0:T(8,128)(2,1)S(1)}, u32[]{:S(2)}, u32[]{:S(2)}) async-start(bf16[32,160,256]{2,1,0:T(8,128)(2,1)} %pack.4), calls=%async_computation.2 | async-start | bytes 5242880 | tf_op jit(solution)/shard_map/all_to_all | solution.py:643
  134.3 4.6 %y_nodes.1 = (bf16[3,512,256]{2,1,0:T(8,128)(2,1)}, f32[6,64,256]{2,1,0:T(8,128)}, bf16[320,256]{1,0:T(8,128)(2,1)S(1)}) custom-call(s32[4]{0:T(128)} %get-tuple-element.59.rows, s32[126,256]{1,0:T(8,128)} %refs_0_.9, bf16[320,256]{1,0:T(8,128)(2,1)S(1)} %get-tuple-element.57.refs_1_, bf16[320,256]{1,0:T(8,128)(2,1)S(1)} %collective-permute-done.4.refs_2_, ...), custom_call_target="tpu_custom_call" | custom-call | flops 603979776 | bytes 6291456 | tf_op jit(solution)/shard_map/y_nodes/pallas_call | solution.py:293
  138.9 2.4 %collective-permute-start.8 = (bf16[320,256]{1,0:T(8,128)(2,1)S(1)}, bf16[320,256]{1,0:T(8,128)(2,1)S(1)}, u32[]{:S(2)}, u32[]{:S(2)}) collective-permute-start(bf16[320,256]{1,0:T(8,128)(2,1)S(1)} %get-tuple-element.60.refs_1_), channel_id=1, source_target_pairs={{0,64},{32,96},{64,0},{96,32},{1,65},{33,97},{65,1},{97,33},{2,66}... | collective-permute-start | bytes 491528 | tf_op jit(solution)/shard_map/ppermute | solution.py:616
  141.3 1.7 collective-permute-start.7
  143.0 13.3 %near.4.refs_11_ = f32[64,4096]{1,0:T(8,128)} custom-call(s32[8,9]{1,0:T(8,128)} %pad_add_fusion.slots, f32[8,1,512]{2,1,0:T(1,128)} %get-tuple-element.62.halves_ref, bf16[8,256,512]{2,1,0:T(8,128)(2,1)} %get-tuple-element.63.targets_hbm, f32[64,4096]{1,0:T(8,128)} %near.3.start_hbm, bf16[32,160,256]{2,1,0:T(8,128)(2,1)} %all-to-all-done.1.block_hbm), custom_call_target="tpu_custom_call" | custom-call | flops 1006632960 | bytes 5767168 | tf_op jit(solution)/shard_map/near/pallas_call | solution.py:588
  156.4 4.3 %z_nodes.1 = (bf16[2,512,256]{2,1,0:T(8,128)(2,1)}, f32[6,64,256]{2,1,0:T(8,128)}, bf16[320,256]{1,0:T(8,128)(2,1)}) custom-call(s32[3]{0:T(128)} %slice_bitcast_fusion.1.rows, s32[126,256]{1,0:T(8,128)} %refs_0_.9, bf16[320,256]{1,0:T(8,128)(2,1)S(1)} %get-tuple-element.60.refs_1_, bf16[320,256]{1,0:T(8,128)(2,1)S(1)} %collective-permute-done.7.refs_2_, ...), custom_call_target="tpu_custom_call" | custom-call | flops 402653184 | bytes 6291456 | tf_op jit(solution)/shard_map/z_nodes/pallas_call | solution.py:293
  160.7 7.3 %down.1.start_hbm = f32[64,4096]{1,0:T(8,128)} custom-call(s32[7]{0:T(128)} %slice_bitcast_fusion.numbers, bf16[2,512,256]{2,1,0:T(8,128)(2,1)} %get-tuple-element.69.refs_0_, f32[6,64,256]{2,1,0:T(8,128)} %get-tuple-element.70.refs_1_, bf16[3,512,256]{2,1,0:T(8,128)(2,1)} %get-tuple-element.71.refs_2_, f32[6,64,256]{2,1,0:T(8,128)} %get-tuple-element.72.refs_3_, ...), custom_call_target="tpu_custom_call" | custom-call | flops 327155712 | bytes 8388608 | tf_op jit(solution)/shard_map/down/pallas_call | solution.py:415
  167.9 2.4 %all-to-all-done.2.block_hbm = bf16[32,160,256]{2,1,0:T(8,128)(2,1)S(1)} async-done(((bf16[32,160,256]{2,1,0:T(8,128)(2,1)}), bf16[32,160,256]{2,1,0:T(8,128)(2,1)S(1)}, u32[]{:S(2)}, u32[]{:S(2)}) %all-to-all-start.2) | async-done | bytes 2621472 | tf_op jit(solution)/shard_map/all_to_all | solution.py:643
  170.4 12.7 %near.5 = f32[64,4096]{1,0:T(8,128)} custom-call(s32[8,9]{1,0:T(8,128)} %pad_add_fusion.slots, f32[8,1,512]{2,1,0:T(1,128)} %get-tuple-element.62.halves_ref, bf16[8,256,512]{2,1,0:T(8,128)(2,1)} %get-tuple-element.63.targets_hbm, f32[64,4096]{1,0:T(8,128)} %down.1.start_hbm, bf16[32,160,256]{2,1,0:T(8,128)(2,1)S(1)} %all-to-all-done.2.block_hbm), custom_call_target="tpu_custom_call" | custom-call | flops 1006632960 | bytes 5767168 | tf_op jit(solution)/shard_map/near/pallas_call | solution.py:588
  (37 shorter events, 11.2 us)
Async XLA Ops:
  6.0 10.8 %copy-start = (bf16[4096,256]{1,0:T(8,128)(2,1)S(1)}, bf16[4096,256]{1,0:T(8,128)(2,1)}, u32[]{:S(2)}) copy-start(bf16[4096,256]{1,0:T(8,128)(2,1)} %points_ref.7) | copy-start | bytes 6291460
  6.0 10.8 %copy-start.1 = (bf16[64,4096]{1,0:T(8,128)(2,1)S(1)}, bf16[64,4096]{1,0:T(8,128)(2,1)}, u32[]{:S(2)}) copy-start(bf16[64,4096]{1,0:T(8,128)(2,1)} %weights_ref.7) | copy-start | bytes 1572868
  6.0 10.8 %copy-start.2 = (s32[8,256]{1,0:T(8,128)S(1)}, s32[8,256]{1,0:T(8,128)}, u32[]{:S(2)}) copy-start(s32[8,256]{1,0:T(8,128)} %chosen_ref.1) | copy-start | bytes 24580
  6.0 76.8 %all-to-all-start = ((bf16[32,320,256]{2,1,0:T(8,128)(2,1)}), bf16[32,320,256]{2,1,0:T(8,128)(2,1)}, u32[]{:S(2)}, u32[]{:S(2)}) async-start(bf16[32,320,256]{2,1,0:T(8,128)(2,1)} %pack.5), calls=%async_computation | async-start | bytes 10485760 | tf_op jit(solution)/shard_map/all_to_all | solution.py:643
  38.0 1.4 collective-permute-start
  42.5 39.5 %collective-permute-start.3 = (bf16[320,256]{1,0:T(8,128)(2,1)S(1)}, bf16[320,256]{1,0:T(8,128)(2,1)S(1)}, u32[]{:S(2)}, u32[]{:S(2)}) collective-permute-start(bf16[320,256]{1,0:T(8,128)(2,1)S(1)} %get-tuple-element.53.refs_1_), channel_id=1, source_target_pairs={{0,6},{1,7},{2,4},{3,5},{4,2},{5,3},{6,0},{7,1},{8,14},{9,15},{10,... | collective-permute-start | bytes 491528 | tf_op jit(solution)/shard_map/ppermute | solution.py:616
  45.5 36.6 %collective-permute-start.2 = (bf16[320,256]{1,0:T(8,128)(2,1)S(1)}, bf16[320,256]{1,0:T(8,128)(2,1)S(1)}, u32[]{:S(2)}, u32[]{:S(2)}) collective-permute-start(bf16[320,256]{1,0:T(8,128)(2,1)S(1)} %get-tuple-element.53.refs_1_), channel_id=1, source_target_pairs={{0,4},{1,5},{2,6},{3,7},{4,0},{5,1},{6,2},{7,3},{8,12},{9,13},{10,... | collective-permute-start | bytes 491528 | tf_op jit(solution)/shard_map/ppermute | solution.py:616
  46.3 36.5 %collective-permute-start.1 = (bf16[320,256]{1,0:T(8,128)(2,1)S(1)}, bf16[320,256]{1,0:T(8,128)(2,1)S(1)}, u32[]{:S(2)}, u32[]{:S(2)}) collective-permute-start(bf16[320,256]{1,0:T(8,128)(2,1)S(1)} %get-tuple-element.53.refs_1_), channel_id=1, source_target_pairs={{0,2},{1,3},{2,0},{3,1},{4,6},{5,7},{6,4},{7,5},{8,10},{9,11},{10,... | collective-permute-start | bytes 491528 | tf_op jit(solution)/shard_map/ppermute | solution.py:616
  82.9 45.9 %all-to-all-start.1 = ((bf16[32,160,256]{2,1,0:T(8,128)(2,1)}), bf16[32,160,256]{2,1,0:T(8,128)(2,1)}, u32[]{:S(2)}, u32[]{:S(2)}) async-start(bf16[32,160,256]{2,1,0:T(8,128)(2,1)} %pack.3), calls=%async_computation.1 | async-start | bytes 5242880 | tf_op jit(solution)/shard_map/all_to_all | solution.py:643
  94.2 34.5 %collective-permute-start.6 = (bf16[320,256]{1,0:T(8,128)(2,1)S(1)}, bf16[320,256]{1,0:T(8,128)(2,1)S(1)}, u32[]{:S(2)}, u32[]{:S(2)}) collective-permute-start(bf16[320,256]{1,0:T(8,128)(2,1)S(1)} %get-tuple-element.57.refs_1_), channel_id=1, source_target_pairs={{0,24},{1,25},{2,26},{3,27},{4,28},{5,29},{6,30},{7,31},{8,16},{9,... | collective-permute-start | bytes 491528 | tf_op jit(solution)/shard_map/ppermute | solution.py:616
  97.2 31.5 %collective-permute-start.5 = (bf16[320,256]{1,0:T(8,128)(2,1)S(1)}, bf16[320,256]{1,0:T(8,128)(2,1)S(1)}, u32[]{:S(2)}, u32[]{:S(2)}) collective-permute-start(bf16[320,256]{1,0:T(8,128)(2,1)S(1)} %get-tuple-element.57.refs_1_), channel_id=1, source_target_pairs={{0,16},{1,17},{2,18},{3,19},{4,20},{5,21},{6,22},{7,23},{8,24},{9,... | collective-permute-start | bytes 491528 | tf_op jit(solution)/shard_map/ppermute | solution.py:616
  98.0 30.7 %collective-permute-start.4 = (bf16[320,256]{1,0:T(8,128)(2,1)S(1)}, bf16[320,256]{1,0:T(8,128)(2,1)S(1)}, u32[]{:S(2)}, u32[]{:S(2)}) collective-permute-start(bf16[320,256]{1,0:T(8,128)(2,1)S(1)} %get-tuple-element.57.refs_1_), channel_id=1, source_target_pairs={{0,8},{1,9},{2,10},{3,11},{4,12},{5,13},{6,14},{7,15},{8,0},{9,1},... | collective-permute-start | bytes 491528 | tf_op jit(solution)/shard_map/ppermute | solution.py:616
  128.7 41.6 %all-to-all-start.2 = ((bf16[32,160,256]{2,1,0:T(8,128)(2,1)}), bf16[32,160,256]{2,1,0:T(8,128)(2,1)S(1)}, u32[]{:S(2)}, u32[]{:S(2)}) async-start(bf16[32,160,256]{2,1,0:T(8,128)(2,1)} %pack.4), calls=%async_computation.2 | async-start | bytes 5242880 | tf_op jit(solution)/shard_map/all_to_all | solution.py:643
  138.9 17.4 %collective-permute-start.9 = (bf16[320,256]{1,0:T(8,128)(2,1)S(1)}, bf16[320,256]{1,0:T(8,128)(2,1)S(1)}, u32[]{:S(2)}, u32[]{:S(2)}) collective-permute-start(bf16[320,256]{1,0:T(8,128)(2,1)S(1)} %get-tuple-element.60.refs_1_), channel_id=1, source_target_pairs={{0,96},{32,64},{64,32},{96,0},{1,97},{33,65},{65,33},{97,1},{2,98}... | collective-permute-start | bytes 491528 | tf_op jit(solution)/shard_map/ppermute | solution.py:616
  138.9 17.4 %collective-permute-start.8 = (bf16[320,256]{1,0:T(8,128)(2,1)S(1)}, bf16[320,256]{1,0:T(8,128)(2,1)S(1)}, u32[]{:S(2)}, u32[]{:S(2)}) collective-permute-start(bf16[320,256]{1,0:T(8,128)(2,1)S(1)} %get-tuple-element.60.refs_1_), channel_id=1, source_target_pairs={{0,64},{32,96},{64,0},{96,32},{1,65},{33,97},{65,1},{97,33},{2,66}... | collective-permute-start | bytes 491528 | tf_op jit(solution)/shard_map/ppermute | solution.py:616
  141.3 15.0 %collective-permute-start.7 = (bf16[320,256]{1,0:T(8,128)(2,1)S(1)}, bf16[320,256]{1,0:T(8,128)(2,1)S(1)}, u32[]{:S(2)}, u32[]{:S(2)}) collective-permute-start(bf16[320,256]{1,0:T(8,128)(2,1)S(1)} %get-tuple-element.60.refs_1_), channel_id=1, source_target_pairs={{0,32},{32,0},{64,96},{96,64},{1,33},{33,1},{65,97},{97,65},{2,34}... | collective-permute-start | bytes 491528 | tf_op jit(solution)/shard_map/ppermute | solution.py:616

commit v2 on v1

--- a/solution.py
+++ b/solution.py
@@ -14,7 +14,7 @@
 LOG2E = 1.4426950408889634
 NT = (((1,), (1,)), ((), ()))
 PARTS = (256, 128, 128)
-GROUP = 1
+GROUP = 2
 
 
 def call(kernel, name, flops, exps, nbytes, vmem=12, **kw):
@@ -86,9 +86,10 @@
 def pack_kernel(leaf_size, first, rows, chosen, points_ref, weights_ref, out_ref, sems):
     classes = weights_ref.shape[0]
     pieces = score_pieces(rows, classes, points_ref.shape[1])
+    group = lax.axis_index("grp") * out_ref.shape[0]
 
     def copies(j):
-        start = pl.multiple_of(chosen[j] * leaf_size + first, 128)
+        start = pl.multiple_of(chosen[group + j] * leaf_size + first, 128)
         made = [
             pltpu.make_async_copy(
                 points_ref.at[pl.ds(start, rows), :],
@@ -110,7 +111,7 @@
         return made
 
     def start(j, carry):
-        @pl.when(chosen[j] >= 0)
+        @pl.when(chosen[group + j] >= 0)
         def _():
             for copy in copies(j):
                 copy.start()
@@ -118,7 +119,7 @@
         return carry
 
     def finish(j, carry):
-        @pl.when(chosen[j] >= 0)
+        @pl.when(chosen[group + j] >= 0)
         def _():
             for copy in copies(j):
                 copy.wait()
@@ -131,7 +132,7 @@
 
 def pack(chosen, points, weights, leaf_size, first, rows):
     classes, width = weights.shape[0], points.shape[1]
-    shape = (chosen.shape[0], rows + rows * classes // width, width)
+    shape = (lax.axis_size("sub"), rows + rows * classes // width, width)
     return call(
         functools.partial(pack_kernel, leaf_size, first, rows),
         "pack",
@@ -439,9 +440,9 @@
 def near_kernel(
     rows, group, resident, slots, halves_ref, targets_hbm, start_hbm, block_hbm, out_ref, *refs
 ):
-    order, leaf_state, block_state, targets_ref, start_ref = refs[:5]
+    order, leaf_state, block_state, targets_ref = refs[:4]
     leaf_sems, block_sems, start_sem = refs[-3:]
-    block_ref = block_hbm if resident else refs[5]
+    block_ref = block_hbm if resident else refs[4]
     leaves, width, size = targets_ref.shape
     sources = block_hbm.shape[0]
     classes = out_ref.shape[0]
@@ -501,12 +502,12 @@
 
     if not resident:
         lax.fori_loop(0, sources, clear, 0)
+    start_copy = pltpu.make_async_copy(start_hbm, out_ref, start_sem)
+    start_copy.start()
     count = lax.fori_loop(0, leaves, list_leaf, 0)
-    start_copy = pltpu.make_async_copy(start_hbm, start_ref, start_sem)
-    start_copy.start()
     steps = (count + group - 1) // group
     lax.fori_loop(count, steps * group, repeat_last, 0)
-    out_ref[...] = jnp.zeros_like(out_ref)
+    start_copy.wait()
 
     def arrive(number):
         leaf = order[number, 0]
@@ -561,8 +562,6 @@
         return carry
 
     lax.fori_loop(0, steps, step, 0)
-    start_copy.wait()
-    out_ref[...] += start_ref[...]
 
 
 def near_part(rows, group, slots, targets, halves, start, blocks, resident, out_type):
@@ -576,7 +575,6 @@
         pltpu.SMEM((leaves,), jnp.int32),
         pltpu.SMEM((blocks.shape[0],), jnp.int32),
         pltpu.VMEM(targets.shape, BF16),
-        pltpu.VMEM(start.shape, F32),
     ]
     if not resident:
         scratch.append(pltpu.VMEM(blocks.shape, BF16))
@@ -627,17 +625,14 @@
     grp_index = lax.axis_index("grp")
     device = grp_index * sub_count + sub_index
 
-    group_first = grp_index * sub_count * leaves
     slot_ids = jnp.arange(slots)
-    group_rows = lax.dynamic_slice_in_dim(near, group_first, sub_count * leaves, 0)
-    group_counts = lax.dynamic_slice_in_dim(counts, group_first, sub_count * leaves, 0)
     owned = (
-        (group_rows // leaves == device)
-        & (slot_ids[None, :] < group_counts[:, None])
+        (near // leaves == device)
+        & (slot_ids[None, :] < counts[:, None])
         & (slot_ids[None, :] > 0)
     )
-    chosen = jnp.where(owned, group_rows - device * leaves, -1).reshape(sub_count, leaves * slots)
-    chosen = jnp.max(chosen, axis=1)
+    chosen = jnp.where(owned, near - device * leaves, -1)
+    chosen = jnp.max(chosen.reshape(sub_count * grp_count, leaves * slots), axis=1)
 
     def send(block):
         return lax.all_to_all(block, "sub", split_axis=0, concat_axis=0, tiled=True)

time: 183 us -> 179 us (0.978); the launches traced: 183 us -> 176 us
  Pallas kernels: 96.8 us -> 76.9 us
  waiting for transfers between devices: 45.8 us -> 59.7 us
    pallas_call x3, Pallas kernels: 42.3 us -> 22.3 us  [near_part(): call(functools.partial(near_kernel, rows, group, resident), 'near', tiles...]
    ppermute x10, waiting for transfers between devices: 43.3 us -> 51.5 us  [swap(): return lax.ppermute(value, axis, pairs)]
    all_to_all x3, waiting for transfers between devices: 2.42 us -> 8.14 us  [send(): return lax.all_to_all(block, 'sub', split_axis=0, concat_axis=0, tiled=True)]
  transfers between devices with their start and end apart: 13 -> 13, of which waited for: 5 -> 6; matrix products, arithmetic and copies ran while one was open for 3% -> 3% of each run, Pallas kernels for 44% -> 37%
where the time goes in v2:
time: 179 us; the launch traced here: 176 us
  Pallas kernels  76.9 us (43%)
  waiting for transfers between devices  59.7 us (33%)
  starting transfers between devices  32.4 us (18%)
  local copies, waits for them, and re-layouts  5.54 us (3%)
    ppermute x10, waiting for transfers between devices, swap(): return lax.ppermute(value, axis, pairs)  51.5 us
    pallas_call x5, Pallas kernels, subtree(): call(functools.partial(subtree_kernel, count, inner, states), name, inner...  26 us
    pallas_call x3, Pallas kernels, near_part(): call(functools.partial(near_kernel, rows, group, resident), 'near', tiles...  22.3 us
    all_to_all x3, starting transfers between devices, send(): return lax.all_to_all(block, 'sub', split_axis=0, concat_axis=0, tiled=True)  20 us
    pallas_call x3, Pallas kernels, pack(): call(functools.partial(pack_kernel, leaf_size, first, rows), 'pack', 0, 0...  12.5 us
    ppermute x10, starting transfers between devices, swap(): return lax.ppermute(value, axis, pairs)  12.5 us
    pallas_call x1, Pallas kernels, leaf_level(): call(leaf_kernel, 'leaf', leaves * 2 * size * (size * (width + classes +...  8.76 us
    all_to_all x3, waiting for transfers between devices, send(): return lax.all_to_all(block, 'sub', split_axis=0, concat_axis=0, tiled=True)  8.14 us
  transfers between devices with their start and end apart: 13, of which 6 were waited for; matrix products, arithmetic and copies ran while one was open for 3% of the time, Pallas kernels for 37%

profile of v2, /device:TPU:96, one launch (start us, length us, event | category | flops | bytes accessed | tf_op | source)
XLA Modules:
  0.0 176.5 jit_solution(7934009409691366959)
XLA Ops:
  1.1 4.2 %pack.5 = bf16[32,320,256]{2,1,0:T(8,128)(2,1)} custom-call(s32[128]{0:T(128)S(1)} %reduce_max.18.chosen, bf16[4096,256]{1,0:T(8,128)(2,1)} %points_ref.7, bf16[64,4096]{1,0:T(8,128)(2,1)} %weights_ref.7), custom_call_target="tpu_custom_call" | custom-call | bytes 10485760 | tf_op jit(solution)/shard_map/pack/pallas_call | solution.py:136
  5.3 7.7 %all-to-all-start = ((bf16[32,320,256]{2,1,0:T(8,128)(2,1)}), bf16[32,320,256]{2,1,0:T(8,128)(2,1)}, u32[]{:S(2)}, u32[]{:S(2)}) async-start(bf16[32,320,256]{2,1,0:T(8,128)(2,1)} %pack.5), calls=%async_computation | async-start | bytes 10485760 | tf_op jit(solution)/shard_map/all_to_all | solution.py:638
  16.1 8.8 %leaf.1 = (f32[64,4096]{1,0:T(8,128)}, bf16[8,256,256]{2,1,0:T(8,128)(2,1)S(1)}, bf16[8,512,256]{2,1,0:T(8,128)(2,1)}, bf16[8,64,256]{2,1,0:T(8,128)(2,1)S(1)}, ...) custom-call(bf16[4096,256]{1,0:T(8,128)(2,1)S(1)} %copy-done, bf16[64,4096]{1,0:T(8,128)(2,1)S(1)} %copy-done.1, ...), custom_call_target="tpu_custom_call" | custom-call | flops 3087007744 | bytes 8388608 | tf_op jit(solution)/shard_map/leaf/pallas_call | solution.py:198
  25.4 9.4 %local.1 = (bf16[7,512,256]{2,1,0:T(8,128)(2,1)}, f32[14,64,256]{2,1,0:T(8,128)}, bf16[320,256]{1,0:T(8,128)(2,1)S(1)}) custom-call(s32[8]{0:T(128)} %iota.10.rows, s32[7,256]{1,0:T(8,128)} %refs_0_.5, bf16[8,256,256]{2,1,0:T(8,128)(2,1)S(1)} %get-tuple-element.44.refs_1_, bf16[8,64,256]{2,1,0:T(8,128)(2,1)S(1)} %get-tuple-element.45.refs_2_), custom_call_target="tpu_custom_call" | custom-call | flops 1409286144 | bytes 6291456 | tf_op jit(solution)/shard_map/local/pallas_call | solution.py:294
  37.5 1.2 collective-permute-done.refs_2_
  38.7 3.1 %core_nodes.1 = (bf16[1,512,256]{2,1,0:T(8,128)(2,1)}, f32[2,64,256]{2,1,0:T(8,128)}, bf16[320,256]{1,0:T(8,128)(2,1)S(1)}) custom-call(s32[2]{0:T(128)} %slice_bitcast_fusion.4.rows, s32[126,256]{1,0:T(8,128)} %refs_0_.9, bf16[320,256]{1,0:T(8,128)(2,1)S(1)} %get-tuple-element.50.refs_1_, bf16[320,256]{1,0:T(8,128)(2,1)S(1)} %collective-permute-done.refs_2_), custom_call_target="tpu_custom_call" | custom-call | flops 201326592 | bytes 6291456 | tf_op jit(solution)/shard_map/core_nodes/pallas_call | solution.py:294
  41.8 2.9 %collective-permute-start.3 = (bf16[320,256]{1,0:T(8,128)(2,1)S(1)}, bf16[320,256]{1,0:T(8,128)(2,1)S(1)}, u32[]{:S(2)}, u32[]{:S(2)}) collective-permute-start(bf16[320,256]{1,0:T(8,128)(2,1)S(1)} %get-tuple-element.53.refs_1_), channel_id=1, source_target_pairs={{0,6},{1,7},{2,4},{3,5},{4,2},{5,3},{6,0},{7,1},{8,14},{9,15},{10,... | collective-permute-start | bytes 491528 | tf_op jit(solution)/shard_map/ppermute | solution.py:614
  45.9 4.1 %pack.4 = bf16[32,160,256]{2,1,0:T(8,128)(2,1)} custom-call(s32[128]{0:T(128)S(1)} %reduce_max.18.chosen, bf16[4096,256]{1,0:T(8,128)(2,1)} %points_ref.7, bf16[64,4096]{1,0:T(8,128)(2,1)} %weights_ref.7), custom_call_target="tpu_custom_call" | custom-call | bytes 5242880 | tf_op jit(solution)/shard_map/pack/pallas_call | solution.py:136
  50.0 4.2 %pack.3 = bf16[32,160,256]{2,1,0:T(8,128)(2,1)} custom-call(s32[128]{0:T(128)S(1)} %reduce_max.18.chosen, bf16[4096,256]{1,0:T(8,128)(2,1)} %points_ref.7, bf16[64,4096]{1,0:T(8,128)(2,1)} %weights_ref.7), custom_call_target="tpu_custom_call" | custom-call | bytes 5242880 | tf_op jit(solution)/shard_map/pack/pallas_call | solution.py:136
  54.2 27.1 %collective-permute-done.3.refs_4_ = bf16[320,256]{1,0:T(8,128)(2,1)S(1)} collective-permute-done((bf16[320,256]{1,0:T(8,128)(2,1)S(1)}, bf16[320,256]{1,0:T(8,128)(2,1)S(1)}, u32[]{:S(2)}, u32[]{:S(2)}) %collective-permute-start.3) | collective-permute-done | bytes 163872 | tf_op jit(solution)/shard_map/ppermute | solution.py:614
  82.1 6.7 %all-to-all-start.1 = ((bf16[32,160,256]{2,1,0:T(8,128)(2,1)}), bf16[32,160,256]{2,1,0:T(8,128)(2,1)}, u32[]{:S(2)}, u32[]{:S(2)}) async-start(bf16[32,160,256]{2,1,0:T(8,128)(2,1)} %pack.3), calls=%async_computation.1 | async-start | bytes 5242880 | tf_op jit(solution)/shard_map/all_to_all | solution.py:638
  88.8 4.6 %x_nodes.1 = (bf16[3,512,256]{2,1,0:T(8,128)(2,1)}, f32[6,64,256]{2,1,0:T(8,128)}, bf16[320,256]{1,0:T(8,128)(2,1)S(1)}) custom-call(s32[4]{0:T(128)} %get-tuple-element.52.rows, s32[126,256]{1,0:T(8,128)} %refs_0_.9, bf16[320,256]{1,0:T(8,128)(2,1)S(1)} %get-tuple-element.53.refs_1_, bf16[320,256]{1,0:T(8,128)(2,1)S(1)} %collective-permute-done.1.refs_2_, ...), custom_call_target="tpu_custom_call" | custom-call | flops 603979776 | bytes 6291456 | tf_op jit(solution)/shard_map/x_nodes/pallas_call | solution.py:294
  93.5 3.0 %collective-permute-start.6 = (bf16[320,256]{1,0:T(8,128)(2,1)S(1)}, bf16[320,256]{1,0:T(8,128)(2,1)S(1)}, u32[]{:S(2)}, u32[]{:S(2)}) collective-permute-start(bf16[320,256]{1,0:T(8,128)(2,1)S(1)} %get-tuple-element.57.refs_1_), channel_id=1, source_target_pairs={{0,24},{1,25},{2,26},{3,27},{4,28},{5,29},{6,30},{7,31},{8,16},{9,... | collective-permute-start | bytes 491528 | tf_op jit(solution)/shard_map/ppermute | solution.py:614
  97.6 8.4 %near.3.start_hbm = f32[64,4096]{1,0:T(8,128)} custom-call(s32[8,9]{1,0:T(8,128)} %pad_add_fusion.slots, f32[8,1,512]{2,1,0:T(1,128)} %get-tuple-element.62.halves_ref, bf16[8,256,512]{2,1,0:T(8,128)(2,1)} %get-tuple-element.63.targets_hbm, f32[64,4096]{1,0:T(8,128)} %get-tuple-element.66.start_hbm, bf16[32,320,256]{2,1,0:T(8,128)(2,1)} %all-to-all-done.block_hbm), custom_call_target="tpu_custom_call" | custom-call | flops 2013265920 | bytes 7340032 | tf_op jit(solution)/shard_map/near/pallas_call | solution.py:586
  106.0 22.0 %collective-permute-done.6.refs_4_ = bf16[320,256]{1,0:T(8,128)(2,1)S(1)} collective-permute-done((bf16[320,256]{1,0:T(8,128)(2,1)S(1)}, bf16[320,256]{1,0:T(8,128)(2,1)S(1)}, u32[]{:S(2)}, u32[]{:S(2)}) %collective-permute-start.6) | collective-permute-done | bytes 163872 | tf_op jit(solution)/shard_map/ppermute | solution.py:614
  128.0 5.6 %all-to-all-start.2 = ((bf16[32,160,256]{2,1,0:T(8,128)(2,1)}), bf16[32,160,256]{2,1,0:T(8,128)(2,1)S(1)}, u32[]{:S(2)}, u32[]{:S(2)}) async-start(bf16[32,160,256]{2,1,0:T(8,128)(2,1)} %pack.4), calls=%async_computation.2 | async-start | bytes 5242880 | tf_op jit(solution)/shard_map/all_to_all | solution.py:638
  133.6 4.6 %y_nodes.1 = (bf16[3,512,256]{2,1,0:T(8,128)(2,1)}, f32[6,64,256]{2,1,0:T(8,128)}, bf16[320,256]{1,0:T(8,128)(2,1)S(1)}) custom-call(s32[4]{0:T(128)} %get-tuple-element.59.rows, s32[126,256]{1,0:T(8,128)} %refs_0_.9, bf16[320,256]{1,0:T(8,128)(2,1)S(1)} %get-tuple-element.57.refs_1_, bf16[320,256]{1,0:T(8,128)(2,1)S(1)} %collective-permute-done.4.refs_2_, ...), custom_call_target="tpu_custom_call" | custom-call | flops 603979776 | bytes 6291456 | tf_op jit(solution)/shard_map/y_nodes/pallas_call | solution.py:294
  138.2 2.4 %collective-permute-start.8 = (bf16[320,256]{1,0:T(8,128)(2,1)S(1)}, bf16[320,256]{1,0:T(8,128)(2,1)S(1)}, u32[]{:S(2)}, u32[]{:S(2)}) collective-permute-start(bf16[320,256]{1,0:T(8,128)(2,1)S(1)} %get-tuple-element.60.refs_1_), channel_id=1, source_target_pairs={{0,64},{32,96},{64,0},{96,32},{1,65},{33,97},{65,1},{97,33},{2,66}... | collective-permute-start | bytes 491528 | tf_op jit(solution)/shard_map/ppermute | solution.py:614
  140.6 1.7 collective-permute-start.7
  142.3 7.2 %near.4.refs_11_ = f32[64,4096]{1,0:T(8,128)} custom-call(s32[8,9]{1,0:T(8,128)} %pad_add_fusion.slots, f32[8,1,512]{2,1,0:T(1,128)} %get-tuple-element.62.halves_ref, bf16[8,256,512]{2,1,0:T(8,128)(2,1)} %get-tuple-element.63.targets_hbm, f32[64,4096]{1,0:T(8,128)} %near.3.start_hbm, bf16[32,160,256]{2,1,0:T(8,128)(2,1)} %all-to-all-done.1.block_hbm), custom_call_target="tpu_custom_call" | custom-call | flops 1006632960 | bytes 5767168 | tf_op jit(solution)/shard_map/near/pallas_call | solution.py:586
  149.9 4.3 %z_nodes.1 = (bf16[2,512,256]{2,1,0:T(8,128)(2,1)}, f32[6,64,256]{2,1,0:T(8,128)}, bf16[320,256]{1,0:T(8,128)(2,1)}) custom-call(s32[3]{0:T(128)} %slice_bitcast_fusion.1.rows, s32[126,256]{1,0:T(8,128)} %refs_0_.9, bf16[320,256]{1,0:T(8,128)(2,1)S(1)} %get-tuple-element.60.refs_1_, bf16[320,256]{1,0:T(8,128)(2,1)S(1)} %collective-permute-done.7.refs_2_, ...), custom_call_target="tpu_custom_call" | custom-call | flops 402653184 | bytes 6291456 | tf_op jit(solution)/shard_map/z_nodes/pallas_call | solution.py:294
  154.2 7.3 %down.1.start_hbm = f32[64,4096]{1,0:T(8,128)} custom-call(s32[7]{0:T(128)} %slice_bitcast_fusion.numbers, bf16[2,512,256]{2,1,0:T(8,128)(2,1)} %get-tuple-element.69.refs_0_, f32[6,64,256]{2,1,0:T(8,128)} %get-tuple-element.70.refs_1_, bf16[3,512,256]{2,1,0:T(8,128)(2,1)} %get-tuple-element.71.refs_2_, f32[6,64,256]{2,1,0:T(8,128)} %get-tuple-element.72.refs_3_, ...), custom_call_target="tpu_custom_call" | custom-call | flops 327155712 | bytes 8388608 | tf_op jit(solution)/shard_map/down/pallas_call | solution.py:416
  161.5 8.1 %all-to-all-done.2.block_hbm = bf16[32,160,256]{2,1,0:T(8,128)(2,1)S(1)} async-done(((bf16[32,160,256]{2,1,0:T(8,128)(2,1)}), bf16[32,160,256]{2,1,0:T(8,128)(2,1)S(1)}, u32[]{:S(2)}, u32[]{:S(2)}) %all-to-all-start.2) | async-done | bytes 2621472 | tf_op jit(solution)/shard_map/all_to_all | solution.py:638
  169.6 6.7 %near.5 = f32[64,4096]{1,0:T(8,128)} custom-call(s32[8,9]{1,0:T(8,128)} %pad_add_fusion.slots, f32[8,1,512]{2,1,0:T(1,128)} %get-tuple-element.62.halves_ref, bf16[8,256,512]{2,1,0:T(8,128)(2,1)} %get-tuple-element.63.targets_hbm, f32[64,4096]{1,0:T(8,128)} %down.1.start_hbm, bf16[32,160,256]{2,1,0:T(8,128)(2,1)S(1)} %all-to-all-done.2.block_hbm), custom_call_target="tpu_custom_call" | custom-call | flops 1006632960 | bytes 5767168 | tf_op jit(solution)/shard_map/near/pallas_call | solution.py:586
  (36 shorter events, 10.9 us)
Async XLA Ops:
  5.3 10.8 %copy-start = (bf16[4096,256]{1,0:T(8,128)(2,1)S(1)}, bf16[4096,256]{1,0:T(8,128)(2,1)}, u32[]{:S(2)}) copy-start(bf16[4096,256]{1,0:T(8,128)(2,1)} %points_ref.7) | copy-start | bytes 6291460
  5.3 10.7 %copy-start.1 = (bf16[64,4096]{1,0:T(8,128)(2,1)S(1)}, bf16[64,4096]{1,0:T(8,128)(2,1)}, u32[]{:S(2)}) copy-start(bf16[64,4096]{1,0:T(8,128)(2,1)} %weights_ref.7) | copy-start | bytes 1572868
  5.3 10.7 %copy-start.2 = (s32[8,256]{1,0:T(8,128)S(1)}, s32[8,256]{1,0:T(8,128)}, u32[]{:S(2)}) copy-start(s32[8,256]{1,0:T(8,128)} %chosen_ref.1) | copy-start | bytes 24580
  5.3 76.8 %all-to-all-start = ((bf16[32,320,256]{2,1,0:T(8,128)(2,1)}), bf16[32,320,256]{2,1,0:T(8,128)(2,1)}, u32[]{:S(2)}, u32[]{:S(2)}) async-start(bf16[32,320,256]{2,1,0:T(8,128)(2,1)} %pack.5), calls=%async_computation | async-start | bytes 10485760 | tf_op jit(solution)/shard_map/all_to_all | solution.py:638
  37.3 1.4 collective-permute-start
  41.8 39.5 %collective-permute-start.3 = (bf16[320,256]{1,0:T(8,128)(2,1)S(1)}, bf16[320,256]{1,0:T(8,128)(2,1)S(1)}, u32[]{:S(2)}, u32[]{:S(2)}) collective-permute-start(bf16[320,256]{1,0:T(8,128)(2,1)S(1)} %get-tuple-element.53.refs_1_), channel_id=1, source_target_pairs={{0,6},{1,7},{2,4},{3,5},{4,2},{5,3},{6,0},{7,1},{8,14},{9,15},{10,... | collective-permute-start | bytes 491528 | tf_op jit(solution)/shard_map/ppermute | solution.py:614
  44.7 36.6 %collective-permute-start.2 = (bf16[320,256]{1,0:T(8,128)(2,1)S(1)}, bf16[320,256]{1,0:T(8,128)(2,1)S(1)}, u32[]{:S(2)}, u32[]{:S(2)}) collective-permute-start(bf16[320,256]{1,0:T(8,128)(2,1)S(1)} %get-tuple-element.53.refs_1_), channel_id=1, source_target_pairs={{0,4},{1,5},{2,6},{3,7},{4,0},{5,1},{6,2},{7,3},{8,12},{9,13},{10,... | collective-permute-start | bytes 491528 | tf_op jit(solution)/shard_map/ppermute | solution.py:614
  45.5 36.5 %collective-permute-start.1 = (bf16[320,256]{1,0:T(8,128)(2,1)S(1)}, bf16[320,256]{1,0:T(8,128)(2,1)S(1)}, u32[]{:S(2)}, u32[]{:S(2)}) collective-permute-start(bf16[320,256]{1,0:T(8,128)(2,1)S(1)} %get-tuple-element.53.refs_1_), channel_id=1, source_target_pairs={{0,2},{1,3},{2,0},{3,1},{4,6},{5,7},{6,4},{7,5},{8,10},{9,11},{10,... | collective-permute-start | bytes 491528 | tf_op jit(solution)/shard_map/ppermute | solution.py:614
  82.1 45.9 %all-to-all-start.1 = ((bf16[32,160,256]{2,1,0:T(8,128)(2,1)}), bf16[32,160,256]{2,1,0:T(8,128)(2,1)}, u32[]{:S(2)}, u32[]{:S(2)}) async-start(bf16[32,160,256]{2,1,0:T(8,128)(2,1)} %pack.3), calls=%async_computation.1 | async-start | bytes 5242880 | tf_op jit(solution)/shard_map/all_to_all | solution.py:638
  93.5 34.5 %collective-permute-start.6 = (bf16[320,256]{1,0:T(8,128)(2,1)S(1)}, bf16[320,256]{1,0:T(8,128)(2,1)S(1)}, u32[]{:S(2)}, u32[]{:S(2)}) collective-permute-start(bf16[320,256]{1,0:T(8,128)(2,1)S(1)} %get-tuple-element.57.refs_1_), channel_id=1, source_target_pairs={{0,24},{1,25},{2,26},{3,27},{4,28},{5,29},{6,30},{7,31},{8,16},{9,... | collective-permute-start | bytes 491528 | tf_op jit(solution)/shard_map/ppermute | solution.py:614
  96.4 31.5 %collective-permute-start.5 = (bf16[320,256]{1,0:T(8,128)(2,1)S(1)}, bf16[320,256]{1,0:T(8,128)(2,1)S(1)}, u32[]{:S(2)}, u32[]{:S(2)}) collective-permute-start(bf16[320,256]{1,0:T(8,128)(2,1)S(1)} %get-tuple-element.57.refs_1_), channel_id=1, source_target_pairs={{0,16},{1,17},{2,18},{3,19},{4,20},{5,21},{6,22},{7,23},{8,24},{9,... | collective-permute-start | bytes 491528 | tf_op jit(solution)/shard_map/ppermute | solution.py:614
  97.3 30.7 %collective-permute-start.4 = (bf16[320,256]{1,0:T(8,128)(2,1)S(1)}, bf16[320,256]{1,0:T(8,128)(2,1)S(1)}, u32[]{:S(2)}, u32[]{:S(2)}) collective-permute-start(bf16[320,256]{1,0:T(8,128)(2,1)S(1)} %get-tuple-element.57.refs_1_), channel_id=1, source_target_pairs={{0,8},{1,9},{2,10},{3,11},{4,12},{5,13},{6,14},{7,15},{8,0},{9,1},... | collective-permute-start | bytes 491528 | tf_op jit(solution)/shard_map/ppermute | solution.py:614
  128.0 41.6 %all-to-all-start.2 = ((bf16[32,160,256]{2,1,0:T(8,128)(2,1)}), bf16[32,160,256]{2,1,0:T(8,128)(2,1)S(1)}, u32[]{:S(2)}, u32[]{:S(2)}) async-start(bf16[32,160,256]{2,1,0:T(8,128)(2,1)} %pack.4), calls=%async_computation.2 | async-start | bytes 5242880 | tf_op jit(solution)/shard_map/all_to_all | solution.py:638
  138.2 11.3 %collective-permute-start.9 = (bf16[320,256]{1,0:T(8,128)(2,1)S(1)}, bf16[320,256]{1,0:T(8,128)(2,1)S(1)}, u32[]{:S(2)}, u32[]{:S(2)}) collective-permute-start(bf16[320,256]{1,0:T(8,128)(2,1)S(1)} %get-tuple-element.60.refs_1_), channel_id=1, source_target_pairs={{0,96},{32,64},{64,32},{96,0},{1,97},{33,65},{65,33},{97,1},{2,98}... | collective-permute-start | bytes 491528 | tf_op jit(solution)/shard_map/ppermute | solution.py:614
  138.2 11.3 %collective-permute-start.8 = (bf16[320,256]{1,0:T(8,128)(2,1)S(1)}, bf16[320,256]{1,0:T(8,128)(2,1)S(1)}, u32[]{:S(2)}, u32[]{:S(2)}) collective-permute-start(bf16[320,256]{1,0:T(8,128)(2,1)S(1)} %get-tuple-element.60.refs_1_), channel_id=1, source_target_pairs={{0,64},{32,96},{64,0},{96,32},{1,65},{33,97},{65,1},{97,33},{2,66}... | collective-permute-start | bytes 491528 | tf_op jit(solution)/shard_map/ppermute | solution.py:614
  140.6 9.3 %collective-permute-start.7 = (bf16[320,256]{1,0:T(8,128)(2,1)S(1)}, bf16[320,256]{1,0:T(8,128)(2,1)S(1)}, u32[]{:S(2)}, u32[]{:S(2)}) collective-permute-start(bf16[320,256]{1,0:T(8,128)(2,1)S(1)} %get-tuple-element.60.refs_1_), channel_id=1, source_target_pairs={{0,32},{32,0},{64,96},{96,64},{1,33},{33,1},{65,97},{97,65},{2,34}... | collective-permute-start | bytes 491528 | tf_op jit(solution)/shard_map/ppermute | solution.py:614

commit v3 on v2

--- a/solution.py
+++ b/solution.py
@@ -342,34 +342,39 @@
     return np.array(table, np.int32), starts, tuple(len(path) for path in paths)
 
 
-def down_kernel(path, stages, numbers, *refs):
-    lifted_hbm, terms_hbm, up_hbm, own_hbm, out_ref = refs[2 * stages : 2 * stages + 5]
-    lifted_ref, terms_ref, up_ref, path_lifted, path_terms, values = refs[2 * stages + 5 : -3]
+def down_kernel(path, top_inner, top_rows, numbers, chosen_ref, *refs):
+    top_count = top_inner + 2
+    top_states = refs[:top_count]
+    stages = refs[top_count : top_count + 2 * (len(path) - 1)]
+    lifted_hbm, terms_hbm, up_hbm, own_hbm, out_ref = refs[top_count + len(stages) :][:5]
+    lifted_ref, terms_ref, up_ref, path_lifted, path_terms, values = refs[-14:-8]
+    top_lifted, top_terms, top_state, nodes, sums = refs[-8:-3]
     path_sems, up_sems, sems = refs[-3:]
     inner, _, rank = lifted_ref.shape
     leaves, size, _ = up_ref.shape
     inverse_rank = 1.0 / rank
 
+    def child_rows(node):
+        return pl.ds(pl.multiple_of((node & 1) * rank, rank), rank)
+
     path_copies = []
-    for stage, steps in enumerate(path):
+    at = path[0]
+    for stage, steps in enumerate(path[1:]):
         for _ in range(steps):
-            at = len(path_copies)
             node = numbers[at]
-            copies = [
-                pltpu.make_async_copy(
-                    refs[2 * stage + 1].at[node], path_terms.at[at], path_sems.at[at, 0]
-                )
-            ]
-            if at > 0:
-                half = pl.ds(pl.multiple_of((node & 1) * rank, rank), rank)
-                copies.append(
+            path_copies.append(
+                [
                     pltpu.make_async_copy(
-                        refs[2 * stage].at[node >> 1, half, :],
+                        stages[2 * stage + 1].at[node], path_terms.at[at], path_sems.at[at, 0]
+                    ),
+                    pltpu.make_async_copy(
+                        stages[2 * stage].at[node >> 1, child_rows(node), :],
                         path_lifted.at[at],
                         path_sems.at[at, 1],
-                    )
-                )
-            path_copies.append(copies)
+                    ),
+                ]
+            )
+            at += 1
     local_copies = [
         pltpu.make_async_copy(terms_hbm, terms_ref, sems.at[0]),
         pltpu.make_async_copy(lifted_hbm, lifted_ref, sems.at[1]),
@@ -385,13 +390,28 @@
     for copy in local_copies + [own_copy] + up_copies:
         copy.start()
 
-    value = None
-    for at, copies in enumerate(path_copies):
+    subtree_kernel(
+        top_count,
+        top_inner,
+        2,
+        top_rows,
+        chosen_ref,
+        *top_states,
+        top_lifted,
+        top_terms,
+        top_state,
+        nodes,
+        sums,
+    )
+    value = top_terms[numbers[0]].astype(BF16)
+    for at in range(1, path[0]):
+        node = numbers[at]
+        child = top_lifted[node >> 1, child_rows(node), :]
+        value = (top_terms[node] + dot_nt(value, child) * inverse_rank).astype(BF16)
+    for at, copies in enumerate(path_copies, path[0]):
         for copy in copies:
             copy.wait()
-        term = path_terms[at]
-        if at > 0:
-            term = term + dot_nt(value, path_lifted[at]) * inverse_rank
+        term = path_terms[at] + dot_nt(value, path_lifted[at]) * inverse_rank
         value = term.astype(BF16)
     values[2 * leaves - 2] = value
     for copy in local_copies:
@@ -408,21 +428,27 @@
         out_ref[:, columns] += dot_nt(values[leaf], up_ref[leaf]) * inverse_rank
 
 
-def down(numbers, path, stages, lifted, terms, up, own):
+def down(top_rows, numbers, table, path, top_states, stages, lifted, terms, up, own):
     leaves, size, rank = up.shape
     classes = own.shape[0]
+    width = table.shape[1]
+    count = len(top_states)
     inputs = [array for stage in stages for array in stage] + [lifted, terms, up, own]
     hbm = pl.BlockSpec(memory_space=pltpu.HBM)
+    vmem = pl.BlockSpec(memory_space=pltpu.VMEM)
+    smem = pl.BlockSpec(memory_space=pltpu.SMEM)
+    state_width = top_states[0].shape[1]
     return call(
-        functools.partial(down_kernel, path, len(stages)),
+        functools.partial(down_kernel, path, count - 2),
         "down",
-        2 * classes * rank * (sum(path) * rank + leaves * size * 2),
-        rank * rank,
+        2 * classes * rank * (sum(path) * rank + leaves * size * 2)
+        + (count - 2) * 2 * rank * rank * (5 * width + 4 * classes),
+        rank * rank * 6,
         8 * 2**20,
         vmem=24,
         out_shape=pltpu.HBM(own.shape, F32),
-        in_specs=[pl.BlockSpec(memory_space=pltpu.SMEM)] + [hbm] * len(inputs),
-        out_specs=pl.BlockSpec(memory_space=pltpu.VMEM),
+        in_specs=[smem, smem, vmem] + [vmem] * count + [hbm] * len(inputs),
+        out_specs=vmem,
         scratch_shapes=[
             pltpu.VMEM(lifted.shape, BF16),
             pltpu.VMEM(terms.shape, F32),
@@ -430,18 +456,29 @@
             pltpu.VMEM((sum(path), rank, rank), BF16),
             pltpu.VMEM((sum(path), classes, rank), F32),
             pltpu.VMEM((2 * leaves, classes, rank), BF16),
+            pltpu.VMEM((count - 2, 2 * rank, rank), BF16),
+            pltpu.VMEM((2 * count - 2, classes, rank), F32),
+            pltpu.VMEM(top_states[0].shape, BF16),
+            pltpu.VMEM((2 * count, rank, state_width), BF16),
+            pltpu.VMEM((2 * count, classes, rank), BF16),
             pltpu.SemaphoreType.DMA((sum(path), 2)),
             pltpu.SemaphoreType.DMA((leaves,)),
             pltpu.SemaphoreType.DMA((3,)),
         ],
-    )(in_hbm(numbers), *(in_hbm(array) for array in inputs))
+    )(
+        in_hbm(top_rows),
+        in_hbm(numbers),
+        in_hbm(table),
+        *top_states,
+        *(in_hbm(array) for array in inputs),
+    )
 
 
 def near_kernel(
     rows, group, resident, slots, halves_ref, targets_hbm, start_hbm, block_hbm, out_ref, *refs
 ):
     order, leaf_state, block_state, targets_ref = refs[:4]
-    leaf_sems, block_sems, start_sem = refs[-3:]
+    leaf_sems, block_sems, start_sems = refs[-3:]
     block_ref = block_hbm if resident else refs[4]
     leaves, width, size = targets_ref.shape
     sources = block_hbm.shape[0]
@@ -453,6 +490,12 @@
             targets_hbm.at[leaf], targets_ref.at[leaf], leaf_sems.at[leaf]
         )
 
+    def start_copy(leaf):
+        columns = pl.ds(pl.multiple_of(leaf * size, size), size)
+        return pltpu.make_async_copy(
+            start_hbm.at[:, columns], out_ref.at[:, columns], start_sems.at[leaf]
+        )
+
     def block_copy(source):
         return pltpu.make_async_copy(
             block_hbm.at[source], block_ref.at[source], block_sems.at[source]
@@ -464,6 +507,7 @@
 
     def list_leaf(number, filled):
         target_copy(number).start()
+        start_copy(number).start()
         leaf_state[number] = 1
 
         def list_slot(slot, carry):
@@ -502,12 +546,9 @@
 
     if not resident:
         lax.fori_loop(0, sources, clear, 0)
-    start_copy = pltpu.make_async_copy(start_hbm, out_ref, start_sem)
-    start_copy.start()
     count = lax.fori_loop(0, leaves, list_leaf, 0)
     steps = (count + group - 1) // group
     lax.fori_loop(count, steps * group, repeat_last, 0)
-    start_copy.wait()
 
     def arrive(number):
         leaf = order[number, 0]
@@ -516,6 +557,7 @@
         def _():
             leaf_state[leaf] = 2
             target_copy(leaf).wait()
+            start_copy(leaf).wait()
 
         for field in (1, 2) if not resident else ():
             source = order[number, field]
@@ -581,7 +623,7 @@
     scratch += [
         pltpu.SemaphoreType.DMA((leaves,)),
         pltpu.SemaphoreType.DMA((blocks.shape[0],)),
-        pltpu.SemaphoreType.DMA,
+        pltpu.SemaphoreType.DMA((leaves,)),
     ]
     return call(
         functools.partial(near_kernel, rows, group, resident),
@@ -702,10 +744,19 @@
     z_states = exchange(state, 3)
     near_slots, _ = lax.optimization_barrier((near_slots, state))
     total = near_sum(1, near_slots, total)
-    z_rows, total = lax.optimization_barrier((stage_rows[3], total))
-    z_stage, _ = climb("z_nodes", z_states, 3, z_rows)
-    stages = [z_stage, y_stage, x_stage, core_stage]
-    total = down(path_nodes, path_lengths, stages, lifted, terms, up, total)
+    stages = [y_stage, x_stage, core_stage]
+    total = down(
+        stage_rows[3],
+        path_nodes,
+        skel_upper,
+        path_lengths,
+        z_states,
+        stages,
+        lifted,
+        terms,
+        up,
+        total,
+    )
     return near_sum(2, near_slots, total, jax.ShapeDtypeStruct)
 
 

time: 179 us -> 179 us (level)
    pallas_call x5 -> x4, Pallas kernels: 26 us -> 21.7 us  [subtree(): call(functools.partial(subtree_kernel, count, inner, states), name, inner...]
    all_to_all x3, waiting for transfers between devices: 8.14 us -> 10.5 us  [send(): return lax.all_to_all(block, 'sub', split_axis=0, concat_axis=0, tiled=True)]
    pallas_call x1, Pallas kernels: 7.26 us -> 9.15 us  [down(): call(functools.partial(down_kernel, path, count - 2), 'down', 2 * classes...]
  transfers between devices with their start and end apart: 13 -> 13, of which waited for: 6 -> 5; matrix products, arithmetic and copies ran while one was open for 3% -> 3% of each run, Pallas kernels for 37% -> 37%
where the time goes in v3:
time: 179 us; the launch traced here: 177 us
  Pallas kernels  75.8 us (42%)
  waiting for transfers between devices  61.1 us (34%)
  starting transfers between devices  32.4 us (18%)
  local copies, waits for them, and re-layouts  5.54 us (3%)
    ppermute x10, waiting for transfers between devices, swap(): return lax.ppermute(value, axis, pairs)  50.5 us
    pallas_call x3, Pallas kernels, near_part(): call(functools.partial(near_kernel, rows, group, resident), 'near', tiles...  23.9 us
    pallas_call x4, Pallas kernels, subtree(): call(functools.partial(subtree_kernel, count, inner, states), name, inner...  21.7 us
    all_to_all x3, starting transfers between devices, send(): return lax.all_to_all(block, 'sub', split_axis=0, concat_axis=0, tiled=True)  19.9 us
    ppermute x10, starting transfers between devices, swap(): return lax.ppermute(value, axis, pairs)  12.5 us
    pallas_call x3, Pallas kernels, pack(): call(functools.partial(pack_kernel, leaf_size, first, rows), 'pack', 0, 0...  12.4 us
    all_to_all x3, waiting for transfers between devices, send(): return lax.all_to_all(block, 'sub', split_axis=0, concat_axis=0, tiled=True)  10.5 us
    pallas_call x1, Pallas kernels, down(): call(functools.partial(down_kernel, path, count - 2), 'down', 2 * classes...  9.15 us
  transfers between devices with their start and end apart: 13, of which 5 were waited for; matrix products, arithmetic and copies ran while one was open for 3% of the time, Pallas kernels for 37%

profile of v3, /device:TPU:96, one launch (start us, length us, event | category | flops | bytes accessed | tf_op | source)
XLA Modules:
  0.0 176.7 jit_solution(16939964501127822297)
XLA Ops:
  1.1 4.2 %pack.5 = bf16[32,320,256]{2,1,0:T(8,128)(2,1)} custom-call(s32[128]{0:T(128)S(1)} %reduce_max.18.chosen, bf16[4096,256]{1,0:T(8,128)(2,1)} %points_ref.7, bf16[64,4096]{1,0:T(8,128)(2,1)} %weights_ref.7), custom_call_target="tpu_custom_call" | custom-call | bytes 10485760 | tf_op jit(solution)/shard_map/pack/pallas_call | solution.py:136
  5.3 7.6 %all-to-all-start = ((bf16[32,320,256]{2,1,0:T(8,128)(2,1)}), bf16[32,320,256]{2,1,0:T(8,128)(2,1)}, u32[]{:S(2)}, u32[]{:S(2)}) async-start(bf16[32,320,256]{2,1,0:T(8,128)(2,1)} %pack.5), calls=%async_computation | async-start | bytes 10485760 | tf_op jit(solution)/shard_map/all_to_all | solution.py:680
  15.9 8.8 %leaf.1 = (f32[64,4096]{1,0:T(8,128)}, bf16[8,256,256]{2,1,0:T(8,128)(2,1)S(1)}, bf16[8,512,256]{2,1,0:T(8,128)(2,1)}, bf16[8,64,256]{2,1,0:T(8,128)(2,1)S(1)}, ...) custom-call(bf16[4096,256]{1,0:T(8,128)(2,1)S(1)} %copy-done, bf16[64,4096]{1,0:T(8,128)(2,1)S(1)} %copy-done.1, ...), custom_call_target="tpu_custom_call" | custom-call | flops 3087007744 | bytes 8388608 | tf_op jit(solution)/shard_map/leaf/pallas_call | solution.py:198
  25.2 9.4 %local.1 = (bf16[7,512,256]{2,1,0:T(8,128)(2,1)}, f32[14,64,256]{2,1,0:T(8,128)}, bf16[320,256]{1,0:T(8,128)(2,1)S(1)}) custom-call(s32[8]{0:T(128)} %iota.10.rows, s32[7,256]{1,0:T(8,128)} %refs_0_.4, bf16[8,256,256]{2,1,0:T(8,128)(2,1)S(1)} %get-tuple-element.40.refs_1_, bf16[8,64,256]{2,1,0:T(8,128)(2,1)S(1)} %get-tuple-element.41.refs_2_), custom_call_target="tpu_custom_call" | custom-call | flops 1409286144 | bytes 6291456 | tf_op jit(solution)/shard_map/local/pallas_call | solution.py:294
  37.3 1.2 collective-permute-done.refs_2_
  38.5 3.1 %core_nodes.1 = (bf16[1,512,256]{2,1,0:T(8,128)(2,1)}, f32[2,64,256]{2,1,0:T(8,128)}, bf16[320,256]{1,0:T(8,128)(2,1)S(1)}) custom-call(s32[2]{0:T(128)} %slice_bitcast_fusion.4.rows, s32[126,256]{1,0:T(8,128)} %chosen_ref.3, bf16[320,256]{1,0:T(8,128)(2,1)S(1)} %get-tuple-element.46.refs_1_, bf16[320,256]{1,0:T(8,128)(2,1)S(1)} %collective-permute-done.refs_2_), custom_call_target="tpu_custom_call" | custom-call | flops 201326592 | bytes 6291456 | tf_op jit(solution)/shard_map/core_nodes/pallas_call | solution.py:294
  41.6 2.9 %collective-permute-start.3 = (bf16[320,256]{1,0:T(8,128)(2,1)S(1)}, bf16[320,256]{1,0:T(8,128)(2,1)S(1)}, u32[]{:S(2)}, u32[]{:S(2)}) collective-permute-start(bf16[320,256]{1,0:T(8,128)(2,1)S(1)} %get-tuple-element.49.refs_1_), channel_id=1, source_target_pairs={{0,6},{1,7},{2,4},{3,5},{4,2},{5,3},{6,0},{7,1},{8,14},{9,15},{10,... | collective-permute-start | bytes 491528 | tf_op jit(solution)/shard_map/ppermute | solution.py:656
  44.5 0.9 collective-permute-start.2
  45.7 4.1 %pack.4 = bf16[32,160,256]{2,1,0:T(8,128)(2,1)} custom-call(s32[128]{0:T(128)S(1)} %reduce_max.18.chosen, bf16[4096,256]{1,0:T(8,128)(2,1)} %points_ref.7, bf16[64,4096]{1,0:T(8,128)(2,1)} %weights_ref.7), custom_call_target="tpu_custom_call" | custom-call | bytes 5242880 | tf_op jit(solution)/shard_map/pack/pallas_call | solution.py:136
  49.8 4.1 %pack.3 = bf16[32,160,256]{2,1,0:T(8,128)(2,1)} custom-call(s32[128]{0:T(128)S(1)} %reduce_max.18.chosen, bf16[4096,256]{1,0:T(8,128)(2,1)} %points_ref.7, bf16[64,4096]{1,0:T(8,128)(2,1)} %weights_ref.7), custom_call_target="tpu_custom_call" | custom-call | bytes 5242880 | tf_op jit(solution)/shard_map/pack/pallas_call | solution.py:136
  53.9 27.2 %collective-permute-done.3.refs_4_ = bf16[320,256]{1,0:T(8,128)(2,1)S(1)} collective-permute-done((bf16[320,256]{1,0:T(8,128)(2,1)S(1)}, bf16[320,256]{1,0:T(8,128)(2,1)S(1)}, u32[]{:S(2)}, u32[]{:S(2)}) %collective-permute-start.3) | collective-permute-done | bytes 163872 | tf_op jit(solution)/shard_map/ppermute | solution.py:656
  82.0 6.7 %all-to-all-start.1 = ((bf16[32,160,256]{2,1,0:T(8,128)(2,1)}), bf16[32,160,256]{2,1,0:T(8,128)(2,1)}, u32[]{:S(2)}, u32[]{:S(2)}) async-start(bf16[32,160,256]{2,1,0:T(8,128)(2,1)} %pack.3), calls=%async_computation.1 | async-start | bytes 5242880 | tf_op jit(solution)/shard_map/all_to_all | solution.py:680
  88.7 4.6 %x_nodes.1 = (bf16[3,512,256]{2,1,0:T(8,128)(2,1)}, f32[6,64,256]{2,1,0:T(8,128)}, bf16[320,256]{1,0:T(8,128)(2,1)S(1)}) custom-call(s32[4]{0:T(128)} %get-tuple-element.48.rows, s32[126,256]{1,0:T(8,128)} %chosen_ref.3, bf16[320,256]{1,0:T(8,128)(2,1)S(1)} %get-tuple-element.49.refs_1_, bf16[320,256]{1,0:T(8,128)(2,1)S(1)} %collective-permute-done.1.refs_2_, ...), custom_call_target="tpu_custom_call" | custom-call | flops 603979776 | bytes 6291456 | tf_op jit(solution)/shard_map/x_nodes/pallas_call | solution.py:294
  93.3 3.0 %collective-permute-start.6 = (bf16[320,256]{1,0:T(8,128)(2,1)S(1)}, bf16[320,256]{1,0:T(8,128)(2,1)S(1)}, u32[]{:S(2)}, u32[]{:S(2)}) collective-permute-start(bf16[320,256]{1,0:T(8,128)(2,1)S(1)} %get-tuple-element.53.refs_1_), channel_id=1, source_target_pairs={{0,24},{1,25},{2,26},{3,27},{4,28},{5,29},{6,30},{7,31},{8,16},{9,... | collective-permute-start | bytes 491528 | tf_op jit(solution)/shard_map/ppermute | solution.py:656
  97.4 9.1 %near.3.start_hbm = f32[64,4096]{1,0:T(8,128)} custom-call(s32[8,9]{1,0:T(8,128)} %pad_add_fusion.slots, f32[8,1,512]{2,1,0:T(1,128)} %get-tuple-element.58.halves_ref, bf16[8,256,512]{2,1,0:T(8,128)(2,1)} %get-tuple-element.59.targets_hbm, f32[64,4096]{1,0:T(8,128)} %get-tuple-element.71.start_hbm, bf16[32,320,256]{2,1,0:T(8,128)(2,1)} %all-to-all-done.block_hbm), custom_call_target="tpu_custom_call" | custom-call | flops 2013265920 | bytes 7340032 | tf_op jit(solution)/shard_map/near/pallas_call | solution.py:628
  106.5 21.3 %collective-permute-done.6.refs_4_ = bf16[320,256]{1,0:T(8,128)(2,1)S(1)} collective-permute-done((bf16[320,256]{1,0:T(8,128)(2,1)S(1)}, bf16[320,256]{1,0:T(8,128)(2,1)S(1)}, u32[]{:S(2)}, u32[]{:S(2)}) %collective-permute-start.6) | collective-permute-done | bytes 163872 | tf_op jit(solution)/shard_map/ppermute | solution.py:656
  127.8 5.6 %all-to-all-start.2 = ((bf16[32,160,256]{2,1,0:T(8,128)(2,1)}), bf16[32,160,256]{2,1,0:T(8,128)(2,1)S(1)}, u32[]{:S(2)}, u32[]{:S(2)}) async-start(bf16[32,160,256]{2,1,0:T(8,128)(2,1)} %pack.4), calls=%async_computation.2 | async-start | bytes 5242880 | tf_op jit(solution)/shard_map/all_to_all | solution.py:680
  133.4 4.6 %y_nodes.1 = (bf16[3,512,256]{2,1,0:T(8,128)(2,1)}, f32[6,64,256]{2,1,0:T(8,128)}, bf16[320,256]{1,0:T(8,128)(2,1)S(1)}) custom-call(s32[4]{0:T(128)} %get-tuple-element.55.rows, s32[126,256]{1,0:T(8,128)} %chosen_ref.3, bf16[320,256]{1,0:T(8,128)(2,1)S(1)} %get-tuple-element.53.refs_1_, bf16[320,256]{1,0:T(8,128)(2,1)S(1)} %collective-permute-done.4.refs_2_, ...), custom_call_target="tpu_custom_call" | custom-call | flops 603979776 | bytes 6291456 | tf_op jit(solution)/shard_map/y_nodes/pallas_call | solution.py:294
  138.0 2.8 %collective-permute-start.8 = (bf16[320,256]{1,0:T(8,128)(2,1)S(1)}, bf16[320,256]{1,0:T(8,128)(2,1)S(1)}, u32[]{:S(2)}, u32[]{:S(2)}) collective-permute-start(bf16[320,256]{1,0:T(8,128)(2,1)S(1)} %get-tuple-element.56.refs_0_), channel_id=1, source_target_pairs={{0,64},{32,96},{64,0},{96,32},{1,65},{33,97},{65,1},{97,33},{2,66}... | collective-permute-start | bytes 491528 | tf_op jit(solution)/shard_map/ppermute | solution.py:656
  140.9 1.2 collective-permute-start.7
  142.1 7.6 %near.4.refs_13_ = f32[64,4096]{1,0:T(8,128)} custom-call(s32[8,9]{1,0:T(8,128)} %pad_add_fusion.slots, f32[8,1,512]{2,1,0:T(1,128)} %get-tuple-element.58.halves_ref, bf16[8,256,512]{2,1,0:T(8,128)(2,1)} %get-tuple-element.59.targets_hbm, f32[64,4096]{1,0:T(8,128)} %near.3.start_hbm, bf16[32,160,256]{2,1,0:T(8,128)(2,1)} %all-to-all-done.1.block_hbm), custom_call_target="tpu_custom_call" | custom-call | flops 1006632960 | bytes 5767168 | tf_op jit(solution)/shard_map/near/pallas_call | solution.py:628
  149.7 9.2 %down.1.start_hbm = f32[64,4096]{1,0:T(8,128)} custom-call(s32[3]{0:T(128)} %slice_bitcast_fusion.1.top_rows, s32[7]{0:T(128)} %slice_bitcast_fusion.numbers, s32[126,256]{1,0:T(8,128)} %chosen_ref.3, bf16[320,256]{1,0:T(8,128)(2,1)S(1)} %get-tuple-element.56.refs_0_, bf16[320,256]{1,0:T(8,128)(2,1)S(1)} %collective-permute-done.7.refs_1_, ...), custom_call_target="tpu_custom_call" | custom-call | flops 729808896 | bytes 8388608 | tf_op jit(solution)/shard_map/down/pallas_call | solution.py:441
  158.9 10.5 %all-to-all-done.2.block_hbm = bf16[32,160,256]{2,1,0:T(8,128)(2,1)S(1)} async-done(((bf16[32,160,256]{2,1,0:T(8,128)(2,1)}), bf16[32,160,256]{2,1,0:T(8,128)(2,1)S(1)}, u32[]{:S(2)}, u32[]{:S(2)}) %all-to-all-start.2) | async-done | bytes 2621472 | tf_op jit(solution)/shard_map/all_to_all | solution.py:680
  169.4 7.1 %near.5 = f32[64,4096]{1,0:T(8,128)} custom-call(s32[8,9]{1,0:T(8,128)} %pad_add_fusion.slots, f32[8,1,512]{2,1,0:T(1,128)} %get-tuple-element.58.halves_ref, bf16[8,256,512]{2,1,0:T(8,128)(2,1)} %get-tuple-element.59.targets_hbm, f32[64,4096]{1,0:T(8,128)} %down.1.start_hbm, bf16[32,160,256]{2,1,0:T(8,128)(2,1)S(1)} %all-to-all-done.2.block_hbm), custom_call_target="tpu_custom_call" | custom-call | flops 1006632960 | bytes 5767168 | tf_op jit(solution)/shard_map/near/pallas_call | solution.py:628
  (35 shorter events, 9.6 us)
Async XLA Ops:
  5.2 10.7 %copy-start = (bf16[4096,256]{1,0:T(8,128)(2,1)S(1)}, bf16[4096,256]{1,0:T(8,128)(2,1)}, u32[]{:S(2)}) copy-start(bf16[4096,256]{1,0:T(8,128)(2,1)} %points_ref.7) | copy-start | bytes 6291460
  5.3 10.7 %copy-start.1 = (bf16[64,4096]{1,0:T(8,128)(2,1)S(1)}, bf16[64,4096]{1,0:T(8,128)(2,1)}, u32[]{:S(2)}) copy-start(bf16[64,4096]{1,0:T(8,128)(2,1)} %weights_ref.7) | copy-start | bytes 1572868
  5.3 10.6 %copy-start.2 = (s32[8,256]{1,0:T(8,128)S(1)}, s32[8,256]{1,0:T(8,128)}, u32[]{:S(2)}) copy-start(s32[8,256]{1,0:T(8,128)} %chosen_ref.2) | copy-start | bytes 24580
  5.3 76.7 %all-to-all-start = ((bf16[32,320,256]{2,1,0:T(8,128)(2,1)}), bf16[32,320,256]{2,1,0:T(8,128)(2,1)}, u32[]{:S(2)}, u32[]{:S(2)}) async-start(bf16[32,320,256]{2,1,0:T(8,128)(2,1)} %pack.5), calls=%async_computation | async-start | bytes 10485760 | tf_op jit(solution)/shard_map/all_to_all | solution.py:680
  37.1 1.4 collective-permute-start
  41.6 39.5 %collective-permute-start.3 = (bf16[320,256]{1,0:T(8,128)(2,1)S(1)}, bf16[320,256]{1,0:T(8,128)(2,1)S(1)}, u32[]{:S(2)}, u32[]{:S(2)}) collective-permute-start(bf16[320,256]{1,0:T(8,128)(2,1)S(1)} %get-tuple-element.49.refs_1_), channel_id=1, source_target_pairs={{0,6},{1,7},{2,4},{3,5},{4,2},{5,3},{6,0},{7,1},{8,14},{9,15},{10,... | collective-permute-start | bytes 491528 | tf_op jit(solution)/shard_map/ppermute | solution.py:656
  44.5 36.6 %collective-permute-start.2 = (bf16[320,256]{1,0:T(8,128)(2,1)S(1)}, bf16[320,256]{1,0:T(8,128)(2,1)S(1)}, u32[]{:S(2)}, u32[]{:S(2)}) collective-permute-start(bf16[320,256]{1,0:T(8,128)(2,1)S(1)} %get-tuple-element.49.refs_1_), channel_id=1, source_target_pairs={{0,4},{1,5},{2,6},{3,7},{4,0},{5,1},{6,2},{7,3},{8,12},{9,13},{10,... | collective-permute-start | bytes 491528 | tf_op jit(solution)/shard_map/ppermute | solution.py:656
  45.4 36.6 %collective-permute-start.1 = (bf16[320,256]{1,0:T(8,128)(2,1)S(1)}, bf16[320,256]{1,0:T(8,128)(2,1)S(1)}, u32[]{:S(2)}, u32[]{:S(2)}) collective-permute-start(bf16[320,256]{1,0:T(8,128)(2,1)S(1)} %get-tuple-element.49.refs_1_), channel_id=1, source_target_pairs={{0,2},{1,3},{2,0},{3,1},{4,6},{5,7},{6,4},{7,5},{8,10},{9,11},{10,... | collective-permute-start | bytes 491528 | tf_op jit(solution)/shard_map/ppermute | solution.py:656
  82.0 45.9 %all-to-all-start.1 = ((bf16[32,160,256]{2,1,0:T(8,128)(2,1)}), bf16[32,160,256]{2,1,0:T(8,128)(2,1)}, u32[]{:S(2)}, u32[]{:S(2)}) async-start(bf16[32,160,256]{2,1,0:T(8,128)(2,1)} %pack.3), calls=%async_computation.1 | async-start | bytes 5242880 | tf_op jit(solution)/shard_map/all_to_all | solution.py:680
  93.3 34.5 %collective-permute-start.6 = (bf16[320,256]{1,0:T(8,128)(2,1)S(1)}, bf16[320,256]{1,0:T(8,128)(2,1)S(1)}, u32[]{:S(2)}, u32[]{:S(2)}) collective-permute-start(bf16[320,256]{1,0:T(8,128)(2,1)S(1)} %get-tuple-element.53.refs_1_), channel_id=1, source_target_pairs={{0,24},{1,25},{2,26},{3,27},{4,28},{5,29},{6,30},{7,31},{8,16},{9,... | collective-permute-start | bytes 491528 | tf_op jit(solution)/shard_map/ppermute | solution.py:656
  96.3 31.5 %collective-permute-start.5 = (bf16[320,256]{1,0:T(8,128)(2,1)S(1)}, bf16[320,256]{1,0:T(8,128)(2,1)S(1)}, u32[]{:S(2)}, u32[]{:S(2)}) collective-permute-start(bf16[320,256]{1,0:T(8,128)(2,1)S(1)} %get-tuple-element.53.refs_1_), channel_id=1, source_target_pairs={{0,16},{1,17},{2,18},{3,19},{4,20},{5,21},{6,22},{7,23},{8,24},{9,... | collective-permute-start | bytes 491528 | tf_op jit(solution)/shard_map/ppermute | solution.py:656
  97.1 30.7 %collective-permute-start.4 = (bf16[320,256]{1,0:T(8,128)(2,1)S(1)}, bf16[320,256]{1,0:T(8,128)(2,1)S(1)}, u32[]{:S(2)}, u32[]{:S(2)}) collective-permute-start(bf16[320,256]{1,0:T(8,128)(2,1)S(1)} %get-tuple-element.53.refs_1_), channel_id=1, source_target_pairs={{0,8},{1,9},{2,10},{3,11},{4,12},{5,13},{6,14},{7,15},{8,0},{9,1},... | collective-permute-start | bytes 491528 | tf_op jit(solution)/shard_map/ppermute | solution.py:656
  127.8 41.6 %all-to-all-start.2 = ((bf16[32,160,256]{2,1,0:T(8,128)(2,1)}), bf16[32,160,256]{2,1,0:T(8,128)(2,1)S(1)}, u32[]{:S(2)}, u32[]{:S(2)}) async-start(bf16[32,160,256]{2,1,0:T(8,128)(2,1)} %pack.4), calls=%async_computation.2 | async-start | bytes 5242880 | tf_op jit(solution)/shard_map/all_to_all | solution.py:680
  138.0 11.7 %collective-permute-start.9 = (bf16[320,256]{1,0:T(8,128)(2,1)S(1)}, bf16[320,256]{1,0:T(8,128)(2,1)S(1)}, u32[]{:S(2)}, u32[]{:S(2)}) collective-permute-start(bf16[320,256]{1,0:T(8,128)(2,1)S(1)} %get-tuple-element.56.refs_0_), channel_id=1, source_target_pairs={{0,96},{32,64},{64,32},{96,0},{1,97},{33,65},{65,33},{97,1},{2,98}... | collective-permute-start | bytes 491528 | tf_op jit(solution)/shard_map/ppermute | solution.py:656
  138.0 11.7 %collective-permute-start.8 = (bf16[320,256]{1,0:T(8,128)(2,1)S(1)}, bf16[320,256]{1,0:T(8,128)(2,1)S(1)}, u32[]{:S(2)}, u32[]{:S(2)}) collective-permute-start(bf16[320,256]{1,0:T(8,128)(2,1)S(1)} %get-tuple-element.56.refs_0_), channel_id=1, source_target_pairs={{0,64},{32,96},{64,0},{96,32},{1,65},{33,97},{65,1},{97,33},{2,66}... | collective-permute-start | bytes 491528 | tf_op jit(solution)/shard_map/ppermute | solution.py:656
  140.9 8.9 %collective-permute-start.7 = (bf16[320,256]{1,0:T(8,128)(2,1)S(1)}, bf16[320,256]{1,0:T(8,128)(2,1)S(1)}, u32[]{:S(2)}, u32[]{:S(2)}) collective-permute-start(bf16[320,256]{1,0:T(8,128)(2,1)S(1)} %get-tuple-element.56.refs_0_), channel_id=1, source_target_pairs={{0,32},{32,0},{64,96},{96,64},{1,33},{33,1},{65,97},{97,65},{2,34}... | collective-permute-start | bytes 491528 | tf_op jit(solution)/shard_map/ppermute | solution.py:656
